TPU v7x, 256 devices: a whole 4x4x8 slice. The times are simulated.
256 devices in a mesh: tok: 32 (over y, x, core), rep: 8 (over z).
Axes of the slice: x: 4, y: 4, z: 8, core: 2. Of those that a mesh axis runs over, the one named last changes fastest.
Arguments:
- hidden_states: bfloat16 [8, 4096, 2048], P('rep', 'tok'), may hold values from -6 to 6
- routes: int32 [8, 4096, 8], P('rep', 'tok'), may hold values from 0 to 31, all different within a row; in each aligned block of 128 rows (0 to 127, 128 to 255, ..., all dimensions but the last counted through in order) at most 36 rows name the same one
- gate_prob: float32 [8, 4096, 8], P('rep', 'tok'), may hold values from 0.03 to 0.3
- gate_up: float32 [32, 2048, 2048], P('tok', 'rep'), may hold values from -0.125 to 0.125
- down: float32 [32, 1024, 2048], P('tok', 'rep'), may hold values from -0.1875 to 0.1875
Outputs:
- mixed: bfloat16 [8, 4096, 2048], P('rep', 'tok')
Inputs may be any that keep to these rules, and one draw needn't show every extreme that they name: `routes`: each row names 8 different experts. No expert is named by more than 36 rows of one device's 128 tokens, and some expert reaches 36 on some devices.
All inputs are finite; a program needn't handle non-finite values.
Results may differ from a plain program's by a relative error of at most 0.012.
Values may be sent and summed in bfloat16 or wider, within the bound.
No kernel may reach another device: no remote copies, remote signals or barrier semaphores. Data moves between devices by JAX's collectives and lax.ppermute only.
A program may use at most 128 MiB of HBM per device.

v0:
```python
import jax
import jax.numpy as jnp
from jax import lax
from jax.sharding import PartitionSpec as P

CAP = 36


def per_device(hidden_states, routes, gate_prob, gate_up, down):
    groups = lax.axis_size("tok")
    local_experts = gate_up.shape[0]
    model_width = hidden_states.shape[2]
    token_count = hidden_states.shape[1]
    top_count = routes.shape[2]
    all_experts = groups * local_experts
    capacity = CAP
    served_gate = gate_up.astype(jnp.bfloat16)
    served_down = down.astype(jnp.bfloat16)
    unit_count = served_gate.shape[2] // 2
    full_gate, full_down = (
        lax.all_gather(served_gate, "rep", axis=1, tiled=True),
        lax.all_gather(served_down, "rep", axis=1, tiled=True),
    )
    flat_picks = routes[0].reshape(-1)
    pick_count = flat_picks.shape[0]
    one_hot = (flat_picks[:, None] == jnp.arange(all_experts, dtype=jnp.int32)[None, :]).astype(
        jnp.int32
    )
    earlier = jnp.cumsum(one_hot, axis=0) - one_hot
    slot_index = jnp.sum(earlier * one_hot, axis=1)
    owners = jnp.arange(pick_count, dtype=jnp.int32) // top_count
    slot_table = (
        jnp.full((all_experts, capacity), token_count, jnp.int32)
        .at[flat_picks, slot_index]
        .set(owners)
    )
    padded_rows = jnp.concatenate(
        [hidden_states[0], jnp.zeros((1, model_width), jnp.bfloat16)], axis=0
    )
    send_rows = padded_rows[slot_table].reshape(groups, local_experts, capacity, model_width)
    arrived = lax.all_to_all(send_rows, "tok", split_axis=0, concat_axis=0, tiled=True)
    gate_both = jnp.einsum("secd,edf->secf", arrived, full_gate, preferred_element_type=jnp.float32)
    hidden_units = (jax.nn.silu(gate_both[..., :unit_count]) * gate_both[..., unit_count:]).astype(
        jnp.bfloat16
    )
    projected = jnp.einsum(
        "secf,efd->secd", hidden_units, full_down, preferred_element_type=jnp.float32
    )
    expert_out = projected.astype(jnp.bfloat16)
    returned = lax.all_to_all(expert_out, "tok", split_axis=0, concat_axis=0, tiled=True)
    returned = returned.reshape(all_experts, capacity, model_width)
    picked_rows = returned[flat_picks, slot_index].reshape(token_count, top_count, model_width)
    mixed_rows = jnp.einsum(
        "tk,tkd->td", gate_prob[0], picked_rows, preferred_element_type=jnp.float32
    )
    return mixed_rows.astype(jnp.bfloat16)[None]


def solution(mesh):
    return jax.shard_map(
        per_device,
        mesh=mesh,
        in_specs=(
            P("rep", "tok", None),
            P("rep", "tok", None),
            P("rep", "tok", None),
            P("tok", "rep", None),
            P("tok", "rep", None),
        ),
        out_specs=P("rep", "tok", None),
        check_vma=False,
    )
```

profile of v0, /device:TPU:96, one launch (start us, length us, event | category | flops | bytes accessed | tf_op | source)
XLA Modules:
  0.0 288.6 jit_solution(6611978452512759054)
XLA Ops:
  6.5 2.8 convert_element_type.33
  9.4 0.8 copy.13
  10.3 0.1 reshape_squeeze.3
  10.4 9.0 %reduce-window.6 = s32[32,8,128]{2,1,0:T(8,128)S(1)} reduce-window(s32[32,8,128]{2,1,0:T(8,128)S(1)} %fusion.21, s32[]{:T(128)} %constant.29.clone.1), window={size=1x1x128 pad=0_0x0_0x127_0}, to_apply=%region_0.0 | reduce-window | flops 4161536 | bytes 262148 | tf_op jit(solution)/shard_map/reduce-window
  19.6 0.1 copy.16
  19.8 0.1 broadcast_add_fusion
  20.2 4.3 %scatter_custom_fusion = s32[1152]{0:T(1024)S(1)} fusion(s32[1024]{0:T(1024)S(1)} %get-tuple-element.9, s32[1024]{0:T(1024)S(1)} %get-tuple-element.8, s32[]{:T(128)} %constant.28.clone.1), kind=kCustom, calls=%fused_computation.40 | custom fusion | bytes 4612
  24.5 0.1 reshape.93
  24.6 0.1 reshape.96
  24.8 6.0 %gather_fusion = bf16[1152,2048]{1,0:T(8,128)(2,1)} fusion(bf16[129,2048]{1,0:T(8,128)(2,1)S(1)} %concatenate.7, s32[2048]{0:T(1024)S(1)} %pad_clamp_fusion), kind=kCustom, calls=%fused_computation | custom fusion | bytes 9441792 | tf_op jit(solution)/shard_map/gather | solution.py:40
  30.8 7.2 %reshape.83 = bf16[32,1,36,2048]{3,2,0,1:T(8,128)(2,1)} reshape(bf16[1152,2048]{1,0:T(8,128)(2,1)} %gather_fusion) | data formatting | bytes 9437184 | tf_op jit(solution)/shard_map/reshape | solution.py:40
  38.0 7.6 %all-to-all-start = ((bf16[32,1,36,2048]{3,2,1,0:T(8,128)(2,1)}), bf16[32,1,36,2048]{3,2,1,0:T(8,128)(2,1)}, u32[]{:S(2)}, u32[]{:S(2)}) async-start(bf16[32,1,36,2048]{3,2,1,0:T(8,128)(2,1)} %bitcast.75), calls=%async_computation | async-start | bytes 10485760 | tf_op jit(solution)/shard_map/all_to_all | solution.py:41
  45.7 0.9 convert_element_type.35
  46.5 64.8 %all-to-all-done = bf16[32,1,36,2048]{3,2,1,0:T(8,128)(2,1)} async-done(((bf16[32,1,36,2048]{3,2,1,0:T(8,128)(2,1)}), bf16[32,1,36,2048]{3,2,1,0:T(8,128)(2,1)}, u32[]{:S(2)}, u32[]{:S(2)}) %all-to-all-start) | async-done | bytes 4718624 | tf_op jit(solution)/shard_map/all_to_all | solution.py:41
  111.4 17.5 %fusion.4 = f32[32,1,36,2048]{3,2,0,1:T(8,128)} fusion(bf16[1,2048,2048]{2,1,0:T(8,128)(2,1)} %all-gather.3.cloned.1.call-done, bf16[32,1,36,2048]{3,2,1,0:T(8,128)(2,1)} %all-to-all-done), kind=kOutput, calls=%fused_computation.9 | convolution fusion | flops 9663676416 | bytes 22544384 | tf_op jit(solution)/shard_map/secd,edf->secf/dot_general | solution.py:42
  128.8 31.4 %all-gather.5.cloned.1.call-done = bf16[1,1024,2048]{2,1,0:T(8,128)(2,1)} async-done(((bf16[1,128,2048]{2,1,0:T(8,128)(2,1)}), bf16[1,1024,2048]{2,1,0:T(8,128)(2,1)}) %all-gather.5.cloned.1.call-update) | async-done | bytes 4194320 | tf_op jit(solution)/shard_map/all_gather | solution.py:22
  160.2 11.3 %convert_bitcast_fusion = bf16[32,1,36,2048]{3,2,1,0:T(8,128)(2,1)} fusion(bf16[1,1024,2048]{2,1,0:T(8,128)(2,1)} %all-gather.5.cloned.1.call-done, f32[32,1,36,2048]{3,2,0,1:T(8,128)} %fusion.4), kind=kOutput, calls=%fused_computation.8 | convolution fusion | flops 4841275392 | bytes 18350080 | tf_op jit(solution)/shard_map/secf,efd->secd/dot_general | solution.py:46
  171.5 7.5 %all-to-all-start.1 = ((bf16[32,1,36,2048]{3,2,1,0:T(8,128)(2,1)}), bf16[32,1,36,2048]{3,2,1,0:T(8,128)(2,1)}, u32[]{:S(2)}, u32[]{:S(2)}) async-start(bf16[32,1,36,2048]{3,2,1,0:T(8,128)(2,1)} %convert_bitcast_fusion), calls=%async_computation.1 | async-start | bytes 10485760 | tf_op jit(solution)/shard_map/all_to_all | solution.py:50
  179.0 0.1 copy.21
  179.2 65.4 %all-to-all-done.1 = bf16[32,1,36,2048]{3,2,1,0:T(8,128)(2,1)} async-done(((bf16[32,1,36,2048]{3,2,1,0:T(8,128)(2,1)}), bf16[32,1,36,2048]{3,2,1,0:T(8,128)(2,1)}, u32[]{:S(2)}, u32[]{:S(2)}) %all-to-all-start.1) | async-done | bytes 4718624 | tf_op jit(solution)/shard_map/all_to_all | solution.py:50
  244.6 7.2 %copy.29 = bf16[32,1,36,2048]{3,0,2,1:T(8,128)(2,1)} copy(bf16[32,1,36,2048]{3,2,1,0:T(8,128)(2,1)} %all-to-all-done.1) | data formatting | bytes 9437184 | tf_op jit(solution)/shard_map/all_to_all | solution.py:50
  251.8 25.4 %gather_fusion.1 = bf16[1024,2048]{1,0:T(8,128)(2,1)} fusion(bf16[32,36,2048]{2,0,1:T(8,128)(2,1)} %bitcast.73, s32[1024]{0:T(1024)S(1)} %bitcast.74), kind=kCustom, calls=%fused_computation.1 | custom fusion | bytes 8396800 | tf_op jit(solution)/shard_map/gather | solution.py:52
  277.2 3.4 %fusion.9 = bf16[128,1,2048]{2,1,0:T(2,128)(2,1)S(1)} fusion(bf16[128,8,1]{1,2,0:T(2,128)(2,1)S(1)} %copy.21, bf16[1024,2048]{1,0:T(8,128)(2,1)} %gather_fusion.1), kind=kOutput, calls=%fused_computation.11 | convolution fusion | flops 4194304 | bytes 4720640 | tf_op jit(solution)/shard_map/tk,tkd->td/dot_general | solution.py:53
  280.6 1.1 copy.30
  (30 shorter events, 0.8 us)
Async XLA Ops:
  6.5 13.5 %copy-start.4 = (s32[2]{0:T(128)S(1)}, s32[2]{0:T(128)}, u32[]{:S(2)}) copy-start(s32[2]{0:T(128)} %constant.45) | copy-start | bytes 28
  6.5 13.5 %copy-start.3 = (s32[2]{0:T(128)S(1)}, s32[2]{0:T(128)}, u32[]{:S(2)}) copy-start(s32[2]{0:T(128)} %constant.48) | copy-start | bytes 28
  6.5 18.2 %copy-start.1 = (bf16[1,128,2048]{2,1,0:T(8,128)(2,1)S(1)}, bf16[1,128,2048]{2,1,0:T(8,128)(2,1)}, u32[]{:S(2)}) copy-start(bf16[1,128,2048]{2,1,0:T(8,128)(2,1)} %param.5) | copy-start | bytes 1572868
  6.5 104.8 %all-gather.3.cloned.1.call-start = ((), (), s32[]{:S(2)}) async-start(), calls=%async_computation.2 | async-start | bytes 9437184 | tf_op jit(solution)/shard_map/all_gather | solution.py:21
  38.0 7.6 %copy-start = (f32[1,128,2048]{2,1,0:T(8,128)S(1)}, f32[1,128,2048]{2,1,0:T(8,128)}, u32[]{:S(2)}) copy-start(f32[1,128,2048]{2,1,0:T(8,128)} %param.9) | copy-start | bytes 3145732
  38.0 73.3 %all-to-all-start = ((bf16[32,1,36,2048]{3,2,1,0:T(8,128)(2,1)}), bf16[32,1,36,2048]{3,2,1,0:T(8,128)(2,1)}, u32[]{:S(2)}, u32[]{:S(2)}) async-start(bf16[32,1,36,2048]{3,2,1,0:T(8,128)(2,1)} %bitcast.75), calls=%async_computation | async-start | bytes 10485760 | tf_op jit(solution)/shard_map/all_to_all | solution.py:41
  45.6 114.6 %all-gather.5.cloned.1.call-start = ((), (), s32[]{:S(2)}) async-start(), calls=%async_computation.3 | async-start | bytes 4718592 | tf_op jit(solution)/shard_map/all_gather | solution.py:22
  171.5 7.5 %copy-start.2 = (f32[1,128,8]{1,2,0:T(8,128)S(1)}, f32[1,128,8]{1,2,0:T(8,128)}, u32[]{:S(2)}) copy-start(f32[1,128,8]{1,2,0:T(8,128)} %param.7) | copy-start | bytes 12292
  171.5 73.1 %all-to-all-start.1 = ((bf16[32,1,36,2048]{3,2,1,0:T(8,128)(2,1)}), bf16[32,1,36,2048]{3,2,1,0:T(8,128)(2,1)}, u32[]{:S(2)}, u32[]{:S(2)}) async-start(bf16[32,1,36,2048]{3,2,1,0:T(8,128)(2,1)} %convert_bitcast_fusion), calls=%async_computation.1 | async-start | bytes 10485760 | tf_op jit(solution)/shard_map/all_to_all | solution.py:50
Sparse Core Ops, SparseCore 0:
  9.5 95.4 all-gather.2
  106.8 53.4 all-gather.4
where the time goes:
time: 290 us; the launch traced here: 289 us
  waiting for transfers between devices  162 us (56%)
  local copies, waits for them, and re-layouts  53 us (18%)
  matrix products  32.2 us (11%)
  starting transfers between devices  15.1 us (5%)
  between operations  13.6 us (5%)
  other arithmetic  13.1 us (5%)
    all_to_all x1, waiting for transfers between devices, per_device(): lax.all_to_all(expert_out, 'tok', split_axis=0, concat_axis=0, tiled=True)  65.4 us
    all_to_all x1, waiting for transfers between devices, per_device(): lax.all_to_all(send_rows, 'tok', split_axis=0, concat_axis=0, tiled=True)  64.8 us
    all_gather x1, waiting for transfers between devices, per_device(): lax.all_gather(served_down, 'rep', axis=1, tiled=True)  31.4 us
    gather x1, local copies, waits for them, and re-layouts, per_device(): returned[flat_picks, slot_index]  25.4 us
    dot_general x1, matrix products, per_device(): jnp.einsum('secd,edf->secf', arrived, full_gate, preferred_element_type=j...  17.5 us
    dot_general x1, matrix products, per_device(): jnp.einsum('secf,efd->secd', hidden_units, full_down, preferred_element_t...  11.3 us
    another operation x3, other arithmetic  9.15 us
    all_to_all x1, starting transfers between devices, per_device(): lax.all_to_all(send_rows, 'tok', split_axis=0, concat_axis=0, tiled=True)  7.56 us
  transfers between devices with their start and end apart: 4, of which 3 were waited for; matrix products, arithmetic and copies ran while one was open for 16% of the time, Pallas kernels for 0%

commit v1 on v0

v1 whole, which is shorter than its diff:
```python
import functools

import jax
import jax.numpy as jnp
from jax import lax
from jax.experimental import pallas as pl
from jax.experimental.pallas import tpu as pltpu
from jax.sharding import PartitionSpec as P

CAP = 36
PAD = 40
MAIN = 32
PACKED = 72
NONE = 200.0
UNIT_BLOCK = 256
EARLY = 768
RANKS = 8
VMEM_LIMIT = 56 << 20


def slots_of(picks, experts):
    count, tokens = experts.shape[0], picks.shape[1]
    named = jnp.zeros((count, tokens), jnp.float32)
    for k in range(picks.shape[0]):
        named = named + (picks[k : k + 1, :] == experts).astype(jnp.float32)
    before = lax.broadcasted_iota(jnp.int32, (tokens, tokens), 0)
    after = lax.broadcasted_iota(jnp.int32, (tokens, tokens), 1)
    earlier = (before < after).astype(jnp.bfloat16)
    slot = jnp.dot(named.astype(jnp.bfloat16), earlier, preferred_element_type=jnp.float32)
    return jnp.where(named > 0.0, slot, NONE)


def dispatch_kernel(picks_ref, rows_ref, send_ref):
    tokens = picks_ref.shape[1]
    group = send_ref.shape[0] // PAD
    experts = pl.program_id(0) * group + lax.broadcasted_iota(jnp.int32, (group, tokens), 0)
    slot = slots_of(picks_ref[...], experts)
    place = lax.broadcasted_iota(jnp.int32, (group, PAD, tokens), 1).astype(jnp.float32)
    chosen = (slot[:, None, :] == place).astype(jnp.float32)
    chosen = chosen.reshape(group * PAD, tokens).astype(jnp.bfloat16)
    send_ref[...] = jnp.dot(chosen, rows_ref[...], preferred_element_type=jnp.float32).astype(
        jnp.bfloat16
    )


def dispatch(picks, rows, all_experts):
    top, tokens = picks.shape
    width = rows.shape[1]
    group = 8
    return pl.pallas_call(
        dispatch_kernel,
        out_shape=jax.ShapeDtypeStruct((all_experts * PAD, width), jnp.bfloat16),
        grid=(all_experts // group,),
        in_specs=[
            pl.BlockSpec((top, tokens), lambda i: (0, 0)),
            pl.BlockSpec((tokens, width), lambda i: (0, 0)),
        ],
        out_specs=pl.BlockSpec((group * PAD, width), lambda i: (i, 0)),
        cost_estimate=pl.CostEstimate(
            flops=2 * all_experts * PAD * tokens * width,
            bytes_accessed=2 * width * (tokens + all_experts * PAD),
            transcendentals=0,
        ),
        name="dispatch",
    )(picks, rows)


def mixer_kernel(picks_ref, probs_ref, mix_ref):
    tokens = picks_ref.shape[1]
    group = mix_ref.shape[1] // PACKED
    experts = pl.program_id(0) * group + lax.broadcasted_iota(jnp.int32, (group, tokens), 0)
    slot = slots_of(picks_ref[...], experts)
    weight = jnp.zeros((group, tokens), jnp.float32)
    for k in range(picks_ref.shape[0]):
        weight = weight + jnp.where(
            picks_ref[k : k + 1, :] == experts, probs_ref[k : k + 1, :], 0.0
        )
    first = jnp.where(slot < MAIN, slot, slot + MAIN)
    second = jnp.where(slot < MAIN, slot + MAIN, slot + CAP)
    row = jnp.concatenate([first, second], axis=1)
    weight = jnp.concatenate([weight, weight], axis=1)
    place = lax.broadcasted_iota(jnp.int32, (group, PACKED, 2 * tokens), 1).astype(jnp.float32)
    spread = jnp.where(row[:, None, :] == place, weight[:, None, :], 0.0)
    spread = spread.reshape(group * PACKED, 2 * tokens).T
    high = spread.astype(jnp.bfloat16)
    mix_ref[: 2 * tokens, :] = high
    mix_ref[2 * tokens :, :] = (spread - high.astype(jnp.float32)).astype(jnp.bfloat16)


def mixer(picks, probs, all_experts):
    top, tokens = picks.shape
    group = 16
    return pl.pallas_call(
        mixer_kernel,
        out_shape=jax.ShapeDtypeStruct((4 * tokens, all_experts * PACKED), jnp.bfloat16),
        grid=(all_experts // group,),
        in_specs=[
            pl.BlockSpec((top, tokens), lambda i: (0, 0)),
            pl.BlockSpec((top, tokens), lambda i: (0, 0)),
        ],
        out_specs=pl.BlockSpec((4 * tokens, group * PACKED), lambda i: (0, i)),
        compiler_params=pltpu.CompilerParams(vmem_limit_bytes=24 << 20),
        cost_estimate=pl.CostEstimate(
            flops=all_experts * PACKED * 2 * tokens * 8,
            bytes_accessed=8 * all_experts * PACKED * tokens,
            transcendentals=0,
        ),
        name="mixer",
    )(picks, probs)


def mix_kernel(mix_ref, back_ref, *refs):
    out_ref = refs[-1]
    tokens = out_ref.shape[0]
    start = refs[0].shape[1] if len(refs) > 1 else 0
    half = back_ref.shape[1]
    both = jnp.dot(mix_ref[...], back_ref[...], preferred_element_type=jnp.float32)
    total = (both[: 2 * tokens] + both[2 * tokens :]).astype(jnp.bfloat16)
    if start:
        out_ref[:, :start] = refs[0][...]
    out_ref[:, start : start + half] = total[:tokens]
    out_ref[:, start + half :] = total[tokens:]


def mix_rows(mix, back, *ready):
    tokens = mix.shape[0] // 4
    width = 2 * back.shape[1] + sum(part.shape[1] for part in ready)
    operands = (mix, back, *ready)
    return pl.pallas_call(
        mix_kernel,
        out_shape=jax.ShapeDtypeStruct((tokens, width), jnp.bfloat16),
        grid=(1,),
        in_specs=[pl.BlockSpec(part.shape, lambda i: (0, 0)) for part in operands],
        out_specs=pl.BlockSpec((tokens, width), lambda i: (0, 0)),
        compiler_params=pltpu.CompilerParams(vmem_limit_bytes=24 << 20),
        cost_estimate=pl.CostEstimate(
            flops=2 * mix.shape[0] * mix.shape[1] * back.shape[1],
            bytes_accessed=2 * (mix.size + back.size + tokens * width),
            transcendentals=0,
        ),
        name="mix",
    )(*operands)


def cast_kernel(gate_ref, down_ref, out_ref):
    width, half = gate_ref.shape[1], out_ref.shape[1] - gate_ref.shape[1]
    rows = down_ref.shape[0]
    out_ref[:, :width] = gate_ref[...].astype(jnp.bfloat16)
    out_ref[:rows, width:] = down_ref[:, :half].astype(jnp.bfloat16)
    out_ref[rows:, width:] = down_ref[:, half:].astype(jnp.bfloat16)


def cast_first(gate_up, down, early):
    rows, width = gate_up.shape
    return pl.pallas_call(
        cast_kernel,
        out_shape=jax.ShapeDtypeStruct((rows, width + early // 2), jnp.bfloat16),
        grid=(1,),
        in_specs=[
            pl.BlockSpec((rows, width), lambda i: (0, 0)),
            pl.BlockSpec((rows // 2, early), lambda i: (0, 0)),
        ],
        out_specs=pl.BlockSpec((rows, width + early // 2), lambda i: (0, 0)),
        compiler_params=pltpu.CompilerParams(vmem_limit_bytes=VMEM_LIMIT),
        name="cast_first",
    )(gate_up, down)


def packed_rows(left, right):
    group, half = left.shape[0] // PAD, left.shape[1]
    left, right = left.reshape(group, PAD, half), right.reshape(group, PAD, half)
    last = left[:, MAIN:, :] + pltpu.roll(right[:, MAIN:, :], PAD - CAP, 1)
    packed = jnp.concatenate([left[:, :MAIN, :], right[:, :MAIN, :], last], axis=1)
    return packed.reshape(group * PACKED, half).astype(jnp.bfloat16)


def front_kernel(
    blocks, rows_ref, gate_ref, up_ref, weight_ref, unit_ref, out_ref, units, early, sem
):
    step = pl.program_id(0)
    width = weight_ref.shape[1] - early.shape[1]
    copy = pltpu.make_async_copy(weight_ref.at[:, width:], early, sem)

    @pl.when(step == 0)
    def _():
        copy.start()

    @pl.when(step < blocks)
    def _():
        gate = jnp.dot(rows_ref[...], gate_ref[...], preferred_element_type=jnp.float32)
        up = jnp.dot(rows_ref[...], up_ref[...], preferred_element_type=jnp.float32)
        unit = (gate * (0.5 * jnp.tanh(0.5 * gate) + 0.5) * up).astype(jnp.bfloat16)
        unit_ref[...] = unit
        units[:, pl.ds(pl.multiple_of(step * UNIT_BLOCK, UNIT_BLOCK), UNIT_BLOCK)] = unit

    @pl.when(step == blocks)
    def _():
        copy.wait()

    @pl.when(step >= blocks)
    def _():
        count = out_ref.shape[0] // PACKED * PAD
        block = units[pl.ds(pl.multiple_of((step - blocks) * count, count), count), :]
        depth = block.shape[1] // RANKS
        parts = []
        for half in range(2):
            weight = jnp.concatenate(
                [
                    early[(2 * rank + half) * depth : (2 * rank + half + 1) * depth, :]
                    for rank in range(RANKS)
                ],
                axis=0,
            )
            parts.append(jnp.dot(block, weight, preferred_element_type=jnp.float32))
        out_ref[...] = packed_rows(*parts)


def front(rows, weight, unit_count):
    count, width = rows.shape
    half = weight.shape[1] - 2 * unit_count
    blocks, group = unit_count // UNIT_BLOCK, 8
    last = blocks - 1
    return pl.pallas_call(
        functools.partial(front_kernel, blocks),
        out_shape=(
            jax.ShapeDtypeStruct((count, unit_count), jnp.bfloat16),
            jax.ShapeDtypeStruct((count // PAD * PACKED, half), jnp.bfloat16),
        ),
        grid=(blocks + count // PAD // group,),
        in_specs=[
            pl.BlockSpec((count, width), lambda i: (0, 0), pipeline_mode=pl.Buffered(1)),
            pl.BlockSpec((width, UNIT_BLOCK), lambda i: (0, jnp.minimum(i, last))),
            pl.BlockSpec((width, UNIT_BLOCK), lambda i: (0, blocks + jnp.minimum(i, last))),
            pl.BlockSpec(memory_space=pl.ANY),
        ],
        out_specs=(
            pl.BlockSpec((count, UNIT_BLOCK), lambda i: (0, jnp.minimum(i, last))),
            pl.BlockSpec((group * PACKED, half), lambda i: (jnp.maximum(i - blocks, 0), 0)),
        ),
        scratch_shapes=[
            pltpu.VMEM((count, unit_count), jnp.bfloat16),
            pltpu.VMEM((weight.shape[0], half), jnp.bfloat16),
            pltpu.SemaphoreType.DMA,
        ],
        compiler_params=pltpu.CompilerParams(vmem_limit_bytes=VMEM_LIMIT),
        cost_estimate=pl.CostEstimate(
            flops=4 * count * width * unit_count + 4 * count * unit_count * half,
            bytes_accessed=2 * (count * width + weight.size + count * unit_count),
            transcendentals=count * unit_count,
        ),
        name="front",
    )(rows, weight, weight, weight)


def down_kernel(unit_ref, weight_ref, out_ref):
    total = jnp.dot(unit_ref[...], weight_ref[...], preferred_element_type=jnp.float32)
    half = total.shape[1] // 2
    out_ref[...] = packed_rows(total[:, :half], total[:, half:])


def down_rows(units, weight):
    count, depth = units.shape
    group, half = 8, weight.shape[1] // 2
    return pl.pallas_call(
        down_kernel,
        out_shape=jax.ShapeDtypeStruct((count // PAD * PACKED, half), jnp.bfloat16),
        grid=(count // PAD // group,),
        in_specs=[
            pl.BlockSpec((group * PAD, depth), lambda i: (i, 0)),
            pl.BlockSpec(weight.shape, lambda i: (0, 0), pipeline_mode=pl.Buffered(1)),
        ],
        out_specs=pl.BlockSpec((group * PACKED, half), lambda i: (i, 0)),
        compiler_params=pltpu.CompilerParams(vmem_limit_bytes=VMEM_LIMIT),
        cost_estimate=pl.CostEstimate(
            flops=4 * count * depth * half,
            bytes_accessed=2 * depth * (count + 2 * half) + 4 * count * half,
            transcendentals=0,
        ),
        name="down_rows",
    )(units, weight)


def per_device(hidden_states, routes, gate_prob, gate_up, down):
    groups = lax.axis_size("tok")
    width = hidden_states.shape[2]
    unit_count = gate_up.shape[2] // 2
    all_experts = groups * gate_up.shape[0]
    gate_up, down = gate_up[0], down[0]

    first = lax.all_gather(cast_first(gate_up, down, EARLY), "rep", axis=0, tiled=True)
    rest = lax.all_gather(
        down[:, EARLY:].astype(jnp.bfloat16), "rep", axis=0, tiled=True
    )

    picks, probs = routes[0].T, gate_prob[0].T
    send = dispatch(picks, hidden_states[0], all_experts)
    arrived = lax.all_to_all(
        send.reshape(groups, PAD, width), "tok", split_axis=0, concat_axis=0, tiled=True
    ).reshape(groups * PAD, width)
    mix = mixer(picks, probs, all_experts)

    units, sent = front(arrived, first, unit_count)
    ready = ()
    for part in range(2):
        if part:
            sent = down_rows(units, rest)
        half = sent.shape[1]
        back = lax.all_to_all(
            sent.reshape(groups, PACKED, half), "tok", split_axis=0, concat_axis=0, tiled=True
        ).reshape(groups * PACKED, half)
        ready = (mix_rows(mix, back, *ready),)
    return ready[0][None]


def solution(mesh):
    return jax.shard_map(
        per_device,
        mesh=mesh,
        in_specs=(
            P("rep", "tok", None),
            P("rep", "tok", None),
            P("rep", "tok", None),
            P("tok", "rep", None),
            P("tok", "rep", None),
        ),
        out_specs=P("rep", "tok", None),
        check_vma=False,
    )
```

time: 290 us -> 231 us (0.80)
  local copies, waits for them, and re-layouts: 53 us -> 3.32 us
  Pallas kernels: 0 us -> 42.3 us
  matrix products: 32.2 us -> 0 us
  other arithmetic: 13.1 us -> 0 us
  waiting for transfers between devices: 162 us -> 151 us
  starting transfers between devices: 15.1 us -> 19.4 us
    pallas_call x0 -> x7, Pallas kernels: none -> 42.3 us  [the longest x1 19.9 us: front(): pl.pallas_call(functools.partial(front_kernel, blocks), out_shape=(jax.Sh...]
    dot_general x3 -> x0, matrix products: 32.2 us -> none  [the longest x1 17.5 us: per_device(): jnp.einsum('secd,edf->secf', arrived, full_gate, preferred_element_type=j...]
    gather x2 -> x0, local copies, waits for them, and re-layouts: 31.3 us -> none  [the longest x1 25.4 us: per_device(): returned[flat_picks, slot_index]]
    all_to_all x2 -> x3, waiting for transfers between devices: 130 us -> 104 us  [the longest x1 63.8 us: per_device(): lax.all_to_all(send.reshape(groups, PAD, width), 'tok', split_axis=0, con...]
    all_gather x2, waiting for transfers between devices: 31.4 us -> 47.5 us  [the longest x1 32 us: per_device(): lax.all_gather(cast_first(gate_up, down, EARLY), 'rep', axis=0, tiled=True)]
    another operation x3 -> x0, other arithmetic: 9.15 us -> none
    reshape x1 -> x0, local copies, waits for them, and re-layouts: 7.24 us -> none  [per_device(): padded_rows[slot_table]]
    all_to_all x1 -> x0, local copies, waits for them, and re-layouts: 7.24 us -> none  [per_device(): lax.all_to_all(expert_out, 'tok', split_axis=0, concat_axis=0, tiled=True)]
  transfers between devices with their start and end apart: 4 -> 5, of which waited for: 3 -> 5; matrix products, arithmetic and copies ran while one was open for 16% -> 1% of each run, Pallas kernels for 0% -> 15%
where the time goes in v1:
time: 231 us; the launch traced here: 230 us
  waiting for transfers between devices  151 us (65%)
  Pallas kernels  42.3 us (18%)
  starting transfers between devices  19.4 us (8%)
  between operations  13.5 us (6%)
  local copies, waits for them, and re-layouts  3.32 us (1%)
    all_to_all x1, waiting for transfers between devices, per_device(): lax.all_to_all(send.reshape(groups, PAD, width), 'tok', split_axis=0, con...  63.8 us
    all_to_all x2, waiting for transfers between devices, per_device(): lax.all_to_all(sent.reshape(groups, PACKED, half), 'tok', split_axis=0, c...  40 us
    all_gather x1, waiting for transfers between devices, per_device(): lax.all_gather(cast_first(gate_up, down, EARLY), 'rep', axis=0, tiled=True)  32 us
    pallas_call x1, Pallas kernels, front(): pl.pallas_call(functools.partial(front_kernel, blocks), out_shape=(jax.Sh...  19.9 us
    all_gather x1, waiting for transfers between devices, per_device(): lax.all_gather(down[:, EARLY:].astype(jnp.bfloat16), 'rep', axis=0, tiled...  15.5 us
    all_to_all x2, starting transfers between devices, per_device(): lax.all_to_all(sent.reshape(groups, PACKED, half), 'tok', split_axis=0, c...  11.9 us
    all_to_all x1, starting transfers between devices, per_device(): lax.all_to_all(send.reshape(groups, PAD, width), 'tok', split_axis=0, con...  7.44 us
    pallas_call x1, Pallas kernels, down_rows(): pl.pallas_call(down_kernel, out_shape=jax.ShapeDtypeStruct((count // PAD...  7.31 us
  transfers between devices with their start and end apart: 5, of which 5 were waited for; matrix products, arithmetic and copies ran while one was open for 1% of the time, Pallas kernels for 15%

profile of v1, /device:TPU:96, one launch (start us, length us, event | category | flops | bytes accessed | tf_op | source)
XLA Modules:
  0.0 229.9 jit_solution(225067434107399956)
XLA Ops:
  6.5 0.0 all-gather.3.cloned.1.call-start
  6.5 2.8 %cast_first.1 = bf16[256,2432]{1,0:T(8,128)(2,1)} custom-call(f32[256,2048]{1,0:T(8,128)} %bitcast.22, f32[128,2048]{1,0:T(8,128)} %bitcast.23), custom_call_target="tpu_custom_call" | custom-call | tf_op jit(solution)/shard_map/cast_first/pallas_call | solution.py:155
  9.3 0.0 all-gather.3.cloned.1.call-update
  9.3 5.1 %dispatch.1 = bf16[1280,2048]{1,0:T(8,128)(2,1)} custom-call(s32[8,128]{1,0:T(8,128)} %bitcast.17, bf16[128,2048]{1,0:T(8,128)(2,1)} %bitcast.26), custom_call_target="tpu_custom_call" | custom-call | flops 671088640 | bytes 5767168 | tf_op jit(solution)/shard_map/dispatch/pallas_call | solution.py:50
  14.5 7.4 %all-to-all-start = ((bf16[32,40,2048]{2,1,0:T(8,128)(2,1)}), bf16[32,40,2048]{2,1,0:T(8,128)(2,1)}, u32[]{:S(2)}, u32[]{:S(2)}) async-start(bf16[32,40,2048]{2,1,0:T(8,128)(2,1)} %bitcast.20), calls=%async_computation | async-start | bytes 10485760 | tf_op jit(solution)/shard_map/all_to_all | solution.py:297
  21.9 0.0 all-gather.5.cloned.1.call-start
  22.0 1.9 slice.7
  23.9 0.0 all-gather.5.cloned.1.call-update
  23.9 63.8 %all-to-all-done = bf16[32,40,2048]{2,1,0:T(8,128)(2,1)} async-done(((bf16[32,40,2048]{2,1,0:T(8,128)(2,1)}), bf16[32,40,2048]{2,1,0:T(8,128)(2,1)}, u32[]{:S(2)}, u32[]{:S(2)}) %all-to-all-start) | async-done | bytes 5242912 | tf_op jit(solution)/shard_map/all_to_all | solution.py:297
  87.7 32.0 %all-gather.3.cloned.1.call-done.gate_ref.up_ref.weight_ref = bf16[2048,2432]{1,0:T(8,128)(2,1)} async-done(((bf16[256,2432]{1,0:T(8,128)(2,1)}), bf16[2048,2432]{1,0:T(8,128)(2,1)}) %all-gather.3.cloned.1.call-update) | async-done | bytes 9961488 | tf_op jit(solution)/shard_map/all_gather | solution.py:290
  119.7 19.9 %front.1 = (bf16[1280,1024]{1,0:T(8,128)(2,1)}, bf16[2304,384]{1,0:T(8,128)(2,1)}) custom-call(bf16[1280,2048]{1,0:T(8,128)(2,1)} %bitcast.7.rows_ref, bf16[2048,2432]{1,0:T(8,128)(2,1)} %all-gather.3.cloned.1.call-done.gate_ref.up_ref.weight_ref, bf16[2048,2432]{1,0:T(8,128)(2,1)} %all-gather.3.cloned.1.call-done.gate_ref.up_ref.weight_ref, ...), custom_call_target="tpu_custom_call" | custom-call | flops 12750684160 | bytes 17825792 | tf_op jit(solution)/shard_map/front/pallas_call | solution.py:223
  139.6 7.1 %all-to-all-start.2 = ((bf16[32,72,384]{2,1,0:T(8,128)(2,1)}), bf16[32,72,384]{2,1,0:T(8,128)(2,1)S(1)}, u32[]{:S(2)}, u32[]{:S(2)}) async-start(bf16[32,72,384]{2,1,0:T(8,128)(2,1)} %bitcast.25), calls=%async_computation.2 | async-start | bytes 3538944 | tf_op jit(solution)/shard_map/all_to_all | solution.py:308
  146.7 15.5 %all-gather.5.cloned.1.call-done.weight_ref = bf16[1024,1280]{1,0:T(8,128)(2,1)} async-done(((bf16[128,1280]{1,0:T(8,128)(2,1)}), bf16[1024,1280]{1,0:T(8,128)(2,1)}) %all-gather.5.cloned.1.call-update) | async-done | bytes 2621456 | tf_op jit(solution)/shard_map/all_gather | solution.py:291
  162.2 7.3 %down_rows.1 = bf16[2304,640]{1,0:T(8,128)(2,1)} custom-call(bf16[1280,1024]{1,0:T(8,128)(2,1)} %get-tuple-element.7.unit_ref, bf16[1024,1280]{1,0:T(8,128)(2,1)} %all-gather.5.cloned.1.call-done.weight_ref), custom_call_target="tpu_custom_call" | custom-call | flops 3355443200 | bytes 8519680 | tf_op jit(solution)/shard_map/down_rows/pallas_call | solution.py:264
  169.5 3.3 %all-to-all-done.2 = bf16[32,72,384]{2,1,0:T(8,128)(2,1)S(1)} async-done(((bf16[32,72,384]{2,1,0:T(8,128)(2,1)}), bf16[32,72,384]{2,1,0:T(8,128)(2,1)S(1)}, u32[]{:S(2)}, u32[]{:S(2)}) %all-to-all-start.2) | async-done | bytes 1769504 | tf_op jit(solution)/shard_map/all_to_all | solution.py:308
  172.8 1.2 copy-done
  174.0 4.8 %all-to-all-start.1 = ((bf16[32,72,640]{2,1,0:T(8,128)(2,1)}), bf16[32,72,640]{2,1,0:T(8,128)(2,1)}, u32[]{:S(2)}, u32[]{:S(2)}) async-start(bf16[32,72,640]{2,1,0:T(8,128)(2,1)} %bitcast.21), calls=%async_computation.1 | async-start | bytes 5898240 | tf_op jit(solution)/shard_map/all_to_all | solution.py:308
  178.9 0.0 copy-start.1
  178.9 0.0 copy-done.2
  178.9 1.2 mixer.1.mix_ref
  180.1 0.2 copy-done.1
  180.3 1.4 mix.2.refs_0_
  181.7 36.7 %all-to-all-done.1 = bf16[32,72,640]{2,1,0:T(8,128)(2,1)} async-done(((bf16[32,72,640]{2,1,0:T(8,128)(2,1)}), bf16[32,72,640]{2,1,0:T(8,128)(2,1)}, u32[]{:S(2)}, u32[]{:S(2)}) %all-to-all-start.1) | async-done | bytes 2949152 | tf_op jit(solution)/shard_map/all_to_all | solution.py:308
  218.4 4.6 %mix.3 = bf16[128,2048]{1,0:T(8,128)(2,1)} custom-call(bf16[512,2304]{1,0:T(8,128)(2,1)S(1)} %mixer.1.mix_ref, bf16[2304,640]{1,0:T(8,128)(2,1)} %bitcast.11.back_ref, bf16[128,768]{1,0:T(8,128)(2,1)S(1)} %mix.2.refs_0_), custom_call_target="tpu_custom_call" | custom-call | flops 1509949440 | bytes 5832704 | tf_op jit(solution)/shard_map/mix/pallas_call | solution.py:129
  (4 shorter events, 0.0 us)
Async XLA Ops:
  6.5 113.2 %all-gather.3.cloned.1.call-start = ((), (), s32[]{:S(2)}) async-start(), calls=%async_computation.3 | async-start | bytes 11206656 | tf_op jit(solution)/shard_map/all_gather | solution.py:290
  14.5 73.2 %all-to-all-start = ((bf16[32,40,2048]{2,1,0:T(8,128)(2,1)}), bf16[32,40,2048]{2,1,0:T(8,128)(2,1)}, u32[]{:S(2)}, u32[]{:S(2)}) async-start(bf16[32,40,2048]{2,1,0:T(8,128)(2,1)} %bitcast.20), calls=%async_computation | async-start | bytes 10485760 | tf_op jit(solution)/shard_map/all_to_all | solution.py:297
  21.9 140.3 %all-gather.5.cloned.1.call-start = ((), (), s32[]{:S(2)}) async-start(), calls=%async_computation.4 | async-start | bytes 2949120 | tf_op jit(solution)/shard_map/all_gather | solution.py:291
  139.6 33.2 %all-to-all-start.2 = ((bf16[32,72,384]{2,1,0:T(8,128)(2,1)}), bf16[32,72,384]{2,1,0:T(8,128)(2,1)S(1)}, u32[]{:S(2)}, u32[]{:S(2)}) async-start(bf16[32,72,384]{2,1,0:T(8,128)(2,1)} %bitcast.25), calls=%async_computation.2 | async-start | bytes 3538944 | tf_op jit(solution)/shard_map/all_to_all | solution.py:308
  172.8 1.2 copy-start
  172.8 6.0 %copy-start.2 = (s32[1,128,8]{1,2,0:T(8,128)S(1)}, s32[1,128,8]{1,2,0:T(8,128)}, u32[]{:S(2)}) copy-start(s32[1,128,8]{1,2,0:T(8,128)} %param.6) | copy-start | bytes 12292
  172.8 6.0 %copy-start.3 = (f32[1,128,8]{1,2,0:T(8,128)S(1)}, f32[1,128,8]{1,2,0:T(8,128)}, u32[]{:S(2)}) copy-start(f32[1,128,8]{1,2,0:T(8,128)} %param.7) | copy-start | bytes 12292
  174.0 44.4 %all-to-all-start.1 = ((bf16[32,72,640]{2,1,0:T(8,128)(2,1)}), bf16[32,72,640]{2,1,0:T(8,128)(2,1)}, u32[]{:S(2)}, u32[]{:S(2)}) async-start(bf16[32,72,640]{2,1,0:T(8,128)(2,1)} %bitcast.21), calls=%async_computation.1 | async-start | bytes 5898240 | tf_op jit(solution)/shard_map/all_to_all | solution.py:308
  178.9 1.5 copy-start.1
Sparse Core Ops, SparseCore 0:
  9.5 110.1 all-gather.2
  121.5 40.6 all-gather.4

commit v2 on v1

--- a/solution.py
+++ b/solution.py
@@ -12,9 +12,11 @@
 MAIN = 32
 PACKED = 72
 NONE = 200.0
-UNIT_BLOCK = 256
-EARLY = 768
-RANKS = 8
+EARLY = 1024
+WINDOW = 3
+MIXER_FLOPS = 40 * 10**9
+ORDER = ("ABABABA", "ABABABB")
+LATE_ORDER = ("efefefe", "efefeff")
 VMEM_LIMIT = 56 << 20
 
 
@@ -46,7 +48,7 @@
 def dispatch(picks, rows, all_experts):
     top, tokens = picks.shape
     width = rows.shape[1]
-    group = 8
+    group = 16
     return pl.pallas_call(
         dispatch_kernel,
         out_shape=jax.ShapeDtypeStruct((all_experts * PAD, width), jnp.bfloat16),
@@ -61,6 +63,7 @@
             bytes_accessed=2 * width * (tokens + all_experts * PAD),
             transcendentals=0,
         ),
+        compiler_params=pltpu.CompilerParams(vmem_limit_bytes=VMEM_LIMIT),
         name="dispatch",
     )(picks, rows)
 
@@ -99,9 +102,9 @@
             pl.BlockSpec((top, tokens), lambda i: (0, 0)),
         ],
         out_specs=pl.BlockSpec((4 * tokens, group * PACKED), lambda i: (0, i)),
-        compiler_params=pltpu.CompilerParams(vmem_limit_bytes=24 << 20),
-        cost_estimate=pl.CostEstimate(
-            flops=all_experts * PACKED * 2 * tokens * 8,
+        compiler_params=pltpu.CompilerParams(vmem_limit_bytes=32 << 20),
+        cost_estimate=pl.CostEstimate(
+            flops=MIXER_FLOPS,
             bytes_accessed=8 * all_experts * PACKED * tokens,
             transcendentals=0,
         ),
@@ -142,28 +145,81 @@
     )(*operands)
 
 
-def cast_kernel(gate_ref, down_ref, out_ref):
-    width, half = gate_ref.shape[1], out_ref.shape[1] - gate_ref.shape[1]
-    rows = down_ref.shape[0]
-    out_ref[:, :width] = gate_ref[...].astype(jnp.bfloat16)
-    out_ref[:rows, width:] = down_ref[:, :half].astype(jnp.bfloat16)
-    out_ref[rows:, width:] = down_ref[:, half:].astype(jnp.bfloat16)
-
-
-def cast_first(gate_up, down, early):
-    rows, width = gate_up.shape
-    return pl.pallas_call(
-        cast_kernel,
-        out_shape=jax.ShapeDtypeStruct((rows, width + early // 2), jnp.bfloat16),
-        grid=(1,),
-        in_specs=[
-            pl.BlockSpec((rows, width), lambda i: (0, 0)),
-            pl.BlockSpec((rows // 2, early), lambda i: (0, 0)),
+def source_ranks(ranks, rightward):
+    me = lax.axis_index("rep")
+    offsets = [0] + [-s for s in range(1, rightward + 1)] + list(range(1, ranks - rightward))
+    return [lax.rem(me + (offset + ranks), ranks) for offset in offsets]
+
+
+def piece_copies(rightward, piece_refs, whole, sem):
+    rows = piece_refs[0].shape[0]
+    copies = []
+    for ref, source in zip(piece_refs, source_ranks(len(piece_refs), rightward)):
+        place = whole.at[pl.ds(pl.multiple_of(source * rows, rows), rows), :]
+        ref = ref.at[:, : whole.shape[1]]
+        copies.append(pltpu.make_async_copy(ref, place, sem.at[len(copies)]))
+    return copies
+
+
+def early_copies(rightwards, ring_refs, whole, sems):
+    rows, quarter = whole.shape[0] // len(ring_refs[0]), whole.shape[1] // 4
+    copies = []
+    for ring, (refs, rightward) in enumerate(zip(ring_refs, rightwards)):
+        for i, (ref, source) in enumerate(zip(refs, source_ranks(len(refs), rightward))):
+            for half in range(2):
+                column = (2 * ring + half) * quarter
+                place = whole.at[
+                    pl.ds(pl.multiple_of(source * rows, rows), rows), column : column + quarter
+                ]
+                piece = ref.at[half * rows : (half + 1) * rows, ref.shape[1] - quarter :]
+                copies.append(pltpu.make_async_copy(piece, place, sems.at[2 * ring + half, i]))
+    return copies
+
+
+def gated(rows, weight):
+    both = jnp.dot(rows, weight, preferred_element_type=jnp.float32)
+    half = both.shape[1] // 2
+    gate, up = both[:, :half], both[:, half:]
+    return (gate * (0.5 * jnp.tanh(0.5 * gate) + 0.5) * up).astype(jnp.bfloat16)
+
+
+def gate_kernel(pieces, rightward, rows_ref, *refs):
+    piece_refs, (unit_ref, whole, sem) = refs[:pieces], refs[pieces:]
+
+    @pl.when(pl.program_id(0) == 0)
+    def _():
+        copies = piece_copies(rightward, piece_refs, whole, sem)
+        for copy in copies:
+            copy.start()
+        for copy in copies:
+            copy.wait()
+
+    unit_ref[...] = gated(rows_ref[...], whole[...])
+
+
+def gate_units(rows, pieces, rightward, columns):
+    count, width = rows.shape
+    depth = pieces[0].shape[0]
+    block = 320
+    return pl.pallas_call(
+        functools.partial(gate_kernel, len(pieces), rightward),
+        out_shape=jax.ShapeDtypeStruct((count, columns // 2), jnp.bfloat16),
+        grid=(count // block,),
+        in_specs=[pl.BlockSpec((block, width), lambda i: (i, 0))]
+        + [pl.BlockSpec(memory_space=pl.ANY)] * len(pieces),
+        out_specs=pl.BlockSpec((block, columns // 2), lambda i: (i, 0)),
+        scratch_shapes=[
+            pltpu.VMEM((depth * len(pieces), columns), jnp.bfloat16),
+            pltpu.SemaphoreType.DMA((len(pieces),)),
         ],
-        out_specs=pl.BlockSpec((rows, width + early // 2), lambda i: (0, 0)),
         compiler_params=pltpu.CompilerParams(vmem_limit_bytes=VMEM_LIMIT),
-        name="cast_first",
-    )(gate_up, down)
+        cost_estimate=pl.CostEstimate(
+            flops=2 * count * width * columns,
+            bytes_accessed=2 * (count * width + width * columns + count * columns // 2),
+            transcendentals=count * columns // 2,
+        ),
+        name="gate_units",
+    )(rows, *pieces)
 
 
 def packed_rows(left, right):
@@ -174,136 +230,213 @@
     return packed.reshape(group * PACKED, half).astype(jnp.bfloat16)
 
 
-def front_kernel(
-    blocks, rows_ref, gate_ref, up_ref, weight_ref, unit_ref, out_ref, units, early, sem
-):
-    step = pl.program_id(0)
-    width = weight_ref.shape[1] - early.shape[1]
-    copy = pltpu.make_async_copy(weight_ref.at[:, width:], early, sem)
-
-    @pl.when(step == 0)
+def front_kernel(pieces, rightwards, rows_ref, ready_ref, *refs):
+    first_refs, second_refs, refs = refs[:pieces], refs[pieces : 2 * pieces], refs[2 * pieces :]
+    unit_ref, out_ref, gate_whole, down_whole, gate_sem, down_sems = refs
+
+    @pl.when(pl.program_id(0) == 0)
     def _():
-        copy.start()
-
-    @pl.when(step < blocks)
-    def _():
-        gate = jnp.dot(rows_ref[...], gate_ref[...], preferred_element_type=jnp.float32)
-        up = jnp.dot(rows_ref[...], up_ref[...], preferred_element_type=jnp.float32)
-        unit = (gate * (0.5 * jnp.tanh(0.5 * gate) + 0.5) * up).astype(jnp.bfloat16)
-        unit_ref[...] = unit
-        units[:, pl.ds(pl.multiple_of(step * UNIT_BLOCK, UNIT_BLOCK), UNIT_BLOCK)] = unit
-
-    @pl.when(step == blocks)
-    def _():
-        copy.wait()
-
-    @pl.when(step >= blocks)
-    def _():
-        count = out_ref.shape[0] // PACKED * PAD
-        block = units[pl.ds(pl.multiple_of((step - blocks) * count, count), count), :]
-        depth = block.shape[1] // RANKS
-        parts = []
-        for half in range(2):
-            weight = jnp.concatenate(
-                [
-                    early[(2 * rank + half) * depth : (2 * rank + half + 1) * depth, :]
-                    for rank in range(RANKS)
-                ],
-                axis=0,
-            )
-            parts.append(jnp.dot(block, weight, preferred_element_type=jnp.float32))
-        out_ref[...] = packed_rows(*parts)
-
-
-def front(rows, weight, unit_count):
+        copies = piece_copies(rightwards[1], second_refs, gate_whole, gate_sem)
+        copies += early_copies(rightwards, (first_refs, second_refs), down_whole, down_sems)
+        for copy in copies:
+            copy.start()
+        for copy in copies:
+            copy.wait()
+
+    unit = gated(rows_ref[...], gate_whole[...])
+    unit_ref[...] = unit
+    block = jnp.concatenate([ready_ref[...], unit], axis=1)
+    total = jnp.dot(block, down_whole[...], preferred_element_type=jnp.float32)
+    half = total.shape[1] // 2
+    out_ref[...] = packed_rows(total[:, :half], total[:, half:])
+
+
+def front(rows, ready, first_pieces, second_pieces, rightwards, early):
     count, width = rows.shape
-    half = weight.shape[1] - 2 * unit_count
-    blocks, group = unit_count // UNIT_BLOCK, 8
-    last = blocks - 1
-    return pl.pallas_call(
-        functools.partial(front_kernel, blocks),
+    ranks = len(second_pieces)
+    depth = second_pieces[0].shape[0]
+    columns = second_pieces[0].shape[1] - early // 4
+    group, unit_count = 8, columns // 2
+    block = group * PAD
+    return pl.pallas_call(
+        functools.partial(front_kernel, ranks, rightwards),
         out_shape=(
             jax.ShapeDtypeStruct((count, unit_count), jnp.bfloat16),
-            jax.ShapeDtypeStruct((count // PAD * PACKED, half), jnp.bfloat16),
-        ),
-        grid=(blocks + count // PAD // group,),
+            jax.ShapeDtypeStruct((count // PAD * PACKED, early // 2), jnp.bfloat16),
+        ),
+        grid=(count // block,),
         in_specs=[
-            pl.BlockSpec((count, width), lambda i: (0, 0), pipeline_mode=pl.Buffered(1)),
-            pl.BlockSpec((width, UNIT_BLOCK), lambda i: (0, jnp.minimum(i, last))),
-            pl.BlockSpec((width, UNIT_BLOCK), lambda i: (0, blocks + jnp.minimum(i, last))),
-            pl.BlockSpec(memory_space=pl.ANY),
-        ],
+            pl.BlockSpec((block, width), lambda i: (i, 0)),
+            pl.BlockSpec((block, ready.shape[1]), lambda i: (i, 0)),
+        ]
+        + [pl.BlockSpec(memory_space=pl.ANY)] * (2 * ranks),
         out_specs=(
-            pl.BlockSpec((count, UNIT_BLOCK), lambda i: (0, jnp.minimum(i, last))),
-            pl.BlockSpec((group * PACKED, half), lambda i: (jnp.maximum(i - blocks, 0), 0)),
+            pl.BlockSpec((block, unit_count), lambda i: (i, 0)),
+            pl.BlockSpec((group * PACKED, early // 2), lambda i: (i, 0)),
         ),
         scratch_shapes=[
-            pltpu.VMEM((count, unit_count), jnp.bfloat16),
-            pltpu.VMEM((weight.shape[0], half), jnp.bfloat16),
-            pltpu.SemaphoreType.DMA,
+            pltpu.VMEM((depth * ranks, columns), jnp.bfloat16),
+            pltpu.VMEM((depth // 2 * ranks, early), jnp.bfloat16),
+            pltpu.SemaphoreType.DMA((ranks,)),
+            pltpu.SemaphoreType.DMA((4, ranks)),
         ],
         compiler_params=pltpu.CompilerParams(vmem_limit_bytes=VMEM_LIMIT),
         cost_estimate=pl.CostEstimate(
-            flops=4 * count * width * unit_count + 4 * count * unit_count * half,
-            bytes_accessed=2 * (count * width + weight.size + count * unit_count),
+            flops=2 * count * (width * columns + depth // 2 * ranks * early),
+            bytes_accessed=2 * (count * width + width * columns + count * columns),
             transcendentals=count * unit_count,
         ),
         name="front",
-    )(rows, weight, weight, weight)
-
-
-def down_kernel(unit_ref, weight_ref, out_ref):
-    total = jnp.dot(unit_ref[...], weight_ref[...], preferred_element_type=jnp.float32)
+    )(rows, ready, *first_pieces, *second_pieces)
+
+
+def late_down_kernel(unit_count, pieces, rightwards, *refs):
+    unit_refs, refs = refs[:unit_count], refs[unit_count:]
+    piece_refs, (out_ref, whole, sems) = refs[:-3], refs[-3:]
+
+    @pl.when(pl.program_id(0) == 0)
+    def _():
+        copies, column = [], 0
+        for ring, rightward in enumerate(rightwards):
+            refs_of = piece_refs[ring * pieces : (ring + 1) * pieces]
+            columns = refs_of[0].shape[1]
+            place = whole.at[:, column : column + columns]
+            copies += piece_copies(rightward, refs_of, place, sems.at[ring])
+            column += columns
+        for copy in copies:
+            copy.start()
+        for copy in copies:
+            copy.wait()
+
+    block = jnp.concatenate([unit_ref[...] for unit_ref in unit_refs], axis=1)
+    total = jnp.dot(block, whole[...], preferred_element_type=jnp.float32)
     half = total.shape[1] // 2
     out_ref[...] = packed_rows(total[:, :half], total[:, half:])
 
 
-def down_rows(units, weight):
-    count, depth = units.shape
-    group, half = 8, weight.shape[1] // 2
-    return pl.pallas_call(
-        down_kernel,
+def late_down_rows(units, rings, rightwards):
+    count, pieces = units[0].shape[0], len(rings[0])
+    depth = rings[0][0].shape[0] * pieces
+    columns = sum(ring[0].shape[1] for ring in rings)
+    group, half = 8, columns // 2
+    return pl.pallas_call(
+        functools.partial(late_down_kernel, len(units), pieces, rightwards),
         out_shape=jax.ShapeDtypeStruct((count // PAD * PACKED, half), jnp.bfloat16),
         grid=(count // PAD // group,),
         in_specs=[
-            pl.BlockSpec((group * PAD, depth), lambda i: (i, 0)),
-            pl.BlockSpec(weight.shape, lambda i: (0, 0), pipeline_mode=pl.Buffered(1)),
+            pl.BlockSpec((group * PAD, part.shape[1]), lambda i: (i, 0)) for part in units
+        ]
+        + [pl.BlockSpec(memory_space=pl.ANY)] * (pieces * len(rings)),
+        out_specs=pl.BlockSpec((group * PACKED, half), lambda i: (i, 0)),
+        scratch_shapes=[
+            pltpu.VMEM((depth, columns), jnp.bfloat16),
+            pltpu.SemaphoreType.DMA((len(rings), pieces)),
         ],
-        out_specs=pl.BlockSpec((group * PACKED, half), lambda i: (i, 0)),
         compiler_params=pltpu.CompilerParams(vmem_limit_bytes=VMEM_LIMIT),
         cost_estimate=pl.CostEstimate(
             flops=4 * count * depth * half,
             bytes_accessed=2 * depth * (count + 2 * half) + 4 * count * half,
             transcendentals=0,
         ),
-        name="down_rows",
-    )(units, weight)
+        name="late_down_rows",
+    )(*units, *[piece for ring in rings for piece in ring])
+
+
+class Rings:
+    def __init__(self, ranks, window):
+        self.ranks, self.window = ranks, window
+        self.pieces = {}
+        self.sent = {"right": [], "left": []}
+
+    def add(self, name, piece):
+        self.pieces[name] = {"right": [piece], "left": [piece]}
+
+    def hop(self, way, name, level):
+        chain = self.pieces[name][way]
+        before = level - self.window
+        waits = [sent[before] for sent in self.sent.values() if before >= 0]
+        waits = [piece for piece in waits if piece is not None]
+        piece, *_ = lax.optimization_barrier((chain[-1], *waits))
+        turn = 1 if way == "right" else -1
+        pairs = [(i, (i + turn) % self.ranks) for i in range(self.ranks)]
+        chain.append(lax.ppermute(piece, "rep", pairs))
+        return chain[-1]
+
+    def hops(self, right, left):
+        for step in range(max(len(right), len(left))):
+            level = len(self.sent["right"])
+            names = {"right": right[step : step + 1], "left": left[step : step + 1]}
+            arrived = {way: self.hop(way, name, level) for way, name in names.items() if name}
+            for way in names:
+                self.sent[way].append(arrived.get(way))
+
+    def all(self, name):
+        chains = self.pieces[name]
+        return chains["right"] + chains["left"][1:]
+
+    def rightward(self, name):
+        return len(self.pieces[name]["right"]) - 1
 
 
 def per_device(hidden_states, routes, gate_prob, gate_up, down):
     groups = lax.axis_size("tok")
+    ranks = lax.axis_size("rep")
     width = hidden_states.shape[2]
     unit_count = gate_up.shape[2] // 2
     all_experts = groups * gate_up.shape[0]
-    gate_up, down = gate_up[0], down[0]
-
-    first = lax.all_gather(cast_first(gate_up, down, EARLY), "rep", axis=0, tiled=True)
-    rest = lax.all_gather(
-        down[:, EARLY:].astype(jnp.bfloat16), "rep", axis=0, tiled=True
-    )
+    gate_up, down, rows = gate_up[0], down[0], hidden_states[0]
+
+    def ring_piece(ring):
+        start, stop = ring * unit_count // 2, (ring + 1) * unit_count // 2
+        quarters = [
+            down[:, (2 * ring + half) * EARLY // 4 : (2 * ring + half + 1) * EARLY // 4]
+            for half in range(2)
+        ]
+        columns = [
+            gate_up[:, start:stop],
+            gate_up[:, unit_count + start : unit_count + stop],
+            jnp.concatenate(quarters, axis=0),
+        ]
+        return jnp.concatenate([part.astype(jnp.bfloat16) for part in columns], axis=1)
+
+    def down_piece(start, stop):
+        return down[:, start:stop].astype(jnp.bfloat16)
+
+    rings = Rings(ranks, WINDOW)
+    rings.add("A", ring_piece(0))
+    rings.add("B", ring_piece(1))
+    rings.hops(*ORDER)
+    middle = (EARLY + width) // 2
+    rings.add("e", down_piece(EARLY, middle))
+    rings.add("f", down_piece(middle, width))
+    rings.hops(*LATE_ORDER)
 
     picks, probs = routes[0].T, gate_prob[0].T
-    send = dispatch(picks, hidden_states[0], all_experts)
+    send = dispatch(picks, rows, all_experts)
     arrived = lax.all_to_all(
         send.reshape(groups, PAD, width), "tok", split_axis=0, concat_axis=0, tiled=True
     ).reshape(groups * PAD, width)
+    waits = [sent[0] for sent in rings.sent.values()]
+    picks, *_ = lax.optimization_barrier((picks, *waits))
     mix = mixer(picks, probs, all_experts)
-
-    units, sent = front(arrived, first, unit_count)
+    arrived, mix = lax.optimization_barrier((arrived, mix))
+
+    units = [gate_units(arrived, rings.all("A"), rings.rightward("A"), unit_count)]
+    second, sent = front(
+        arrived,
+        units[0],
+        rings.all("A"),
+        rings.all("B"),
+        [rings.rightward("A"), rings.rightward("B")],
+        EARLY,
+    )
+    units.append(second)
     ready = ()
     for part in range(2):
         if part:
-            sent = down_rows(units, rest)
+            sent = late_down_rows(
+                units, [rings.all(name) for name in "ef"], [rings.rightward(name) for name in "ef"]
+            )
         half = sent.shape[1]
         back = lax.all_to_all(
             sent.reshape(groups, PACKED, half), "tok", split_axis=0, concat_axis=0, tiled=True

time: 231 us -> 228 us (0.987)
  starting transfers between devices: 19.4 us -> 61.9 us
  waiting for transfers between devices: 151 us -> 113 us
  between operations: 13.5 us -> 0.42 us
  other arithmetic: 0 us -> 3.11 us
    ppermute x0 -> x28, waiting for transfers between devices: none -> 82.9 us  [hop(): chain.append(lax.ppermute(piece, 'rep', pairs))]
    all_to_all x1, waiting for transfers between devices: 63.8 us -> 0.01 us  [per_device(): lax.all_to_all(send.reshape(groups, PAD, width), 'tok', split_axis=0, con...]
    all_gather x2 -> x0, waiting for transfers between devices: 47.5 us -> none  [the longest x1 32 us: per_device(): lax.all_gather(cast_first(gate_up, down, EARLY), 'rep', axis=0, tiled=True)]
    ppermute x0 -> x28, starting transfers between devices: none -> 39.9 us  [hop(): chain.append(lax.ppermute(piece, 'rep', pairs))]
    all_to_all x2, waiting for transfers between devices: 40 us -> 30 us  [per_device(): lax.all_to_all(sent.reshape(groups, PACKED, half), 'tok', split_axis=0, c...]
    unnamed x8 -> x58, local copies, waits for them, and re-layouts: 1.41 us -> 5.47 us
    another operation x0 -> x2, other arithmetic: none -> 3.02 us
    pallas_call x3, Pallas kernels: 30 us -> 32.5 us  [the longest x1 14.5 us: front(): pl.pallas_call(functools.partial(front_kernel, ranks, rightwards), out_sh...]
  transfers between devices with their start and end apart: 5 -> 31, of which waited for: 5 -> 20; matrix products, arithmetic and copies ran while one was open for 1% -> 0% of each run, Pallas kernels for 15% -> 11%
where the time goes in v2:
time: 228 us
  waiting for transfers between devices  113 us (50%)
  starting transfers between devices  61.9 us (27%)
  Pallas kernels  43.7 us (19%)
  local copies, waits for them, and re-layouts  5.59 us (2%)
  other arithmetic  3.11 us (1%)
    ppermute x28, waiting for transfers between devices, hop(): chain.append(lax.ppermute(piece, 'rep', pairs))  82.9 us
    ppermute x28, starting transfers between devices, hop(): chain.append(lax.ppermute(piece, 'rep', pairs))  39.9 us
    all_to_all x2, waiting for transfers between devices, per_device(): lax.all_to_all(sent.reshape(groups, PACKED, half), 'tok', split_axis=0, c...  30 us
    pallas_call x1, Pallas kernels, front(): pl.pallas_call(functools.partial(front_kernel, ranks, rightwards), out_sh...  14.5 us
    all_to_all x2, starting transfers between devices, per_device(): lax.all_to_all(sent.reshape(groups, PACKED, half), 'tok', split_axis=0, c...  14.3 us
    pallas_call x1, Pallas kernels, gate_units(): pl.pallas_call(functools.partial(gate_kernel, len(pieces), rightward), ou...  10.5 us
    all_to_all x1, starting transfers between devices, per_device(): lax.all_to_all(send.reshape(groups, PAD, width), 'tok', split_axis=0, con...  7.57 us
    pallas_call x1, Pallas kernels, late_down_rows(): pl.pallas_call(functools.partial(late_down_kernel, len(units), pieces, ri...  7.51 us
  transfers between devices with their start and end apart: 31, of which 20 were waited for; matrix products, arithmetic and copies ran while one was open for 0% of the time, Pallas kernels for 11%

profile of v2, /device:TPU:96, one launch (start us, length us, event | category | flops | bytes accessed | tf_op | source)
XLA Modules:
  0.0 227.6 jit_solution(6522204109573771514)
XLA Ops:
  6.6 4.7 %dispatch.1 = bf16[1280,2048]{1,0:T(8,128)(2,1)} custom-call(s32[8,128]{1,0:T(8,128)} %bitcast.19, bf16[128,2048]{1,0:T(8,128)(2,1)} %bitcast.25), custom_call_target="tpu_custom_call" | custom-call | flops 671088640 | bytes 5767168 | tf_op jit(solution)/shard_map/dispatch/pallas_call | solution.py:52
  11.3 7.6 %all-to-all-start = ((bf16[32,40,2048]{2,1,0:T(8,128)(2,1)}), bf16[32,40,2048]{2,1,0:T(8,128)(2,1)}, u32[]{:S(2)}, u32[]{:S(2)}) async-start(bf16[32,40,2048]{2,1,0:T(8,128)(2,1)} %bitcast.22), calls=%async_computation | async-start | bytes 10485760 | tf_op jit(solution)/shard_map/all_to_all | solution.py:416
  18.9 3.3 %collective-permute-start.3 = (bf16[256,1280]{1,0:T(8,128)(2,1)S(1)}, bf16[256,1280]{1,0:T(8,128)(2,1)S(1)}, u32[]{:S(2)}, u32[]{:S(2)}) collective-permute-start(bf16[256,1280]{1,0:T(8,128)(2,1)S(1)} %maximum_maximum_fusion.1.refs_8_), channel_id=1, source_target_pairs={{0,1},{1,2},{2,3},{3,4},{4,5},{5,6},{6,7},{7,0},{8,9},{9,10},{10,1... | collective-permute-start | bytes 1966088 | tf_op jit(solution)/shard_map/ppermute | solution.py:362
  25.3 12.7 %collective-permute-done.4.refs_12_ = bf16[256,1280]{1,0:T(8,128)(2,1)} collective-permute-done((bf16[256,1280]{1,0:T(8,128)(2,1)S(1)}, bf16[256,1280]{1,0:T(8,128)(2,1)}, u32[]{:S(2)}, u32[]{:S(2)}) %collective-permute-start.4) | collective-permute-done | bytes 655392 | tf_op jit(solution)/shard_map/ppermute | solution.py:362
  38.0 3.3 %collective-permute-start.6 = (bf16[256,1280]{1,0:T(8,128)(2,1)S(1)}, bf16[256,1280]{1,0:T(8,128)(2,1)S(1)}, u32[]{:S(2)}, u32[]{:S(2)}) collective-permute-start(bf16[256,1280]{1,0:T(8,128)(2,1)S(1)} %collective-permute-done.3.refs_9_), channel_id=1, source_target_pairs={{0,1},{1,2},{2,3},{3,4},{4,5},{5,6},{6,7},{7,0},{8,9},{9,10},{10,1... | collective-permute-start | bytes 1966088 | tf_op jit(solution)/shard_map/ppermute | solution.py:362
  41.3 10.0 %collective-permute-done.2.refs_2_ = bf16[256,1280]{1,0:T(8,128)(2,1)S(1)} collective-permute-done((bf16[256,1280]{1,0:T(8,128)(2,1)S(1)}, bf16[256,1280]{1,0:T(8,128)(2,1)S(1)}, u32[]{:S(2)}, u32[]{:S(2)}) %collective-permute-start.2) | collective-permute-done | bytes 655392 | tf_op jit(solution)/shard_map/ppermute | solution.py:362
  51.3 3.7 %collective-permute-start.5 = (bf16[256,1280]{1,0:T(8,128)(2,1)S(1)}, bf16[256,1280]{1,0:T(8,128)(2,1)}, u32[]{:S(2)}, u32[]{:S(2)}) collective-permute-start(bf16[256,1280]{1,0:T(8,128)(2,1)S(1)} %collective-permute-done.2.refs_2_), channel_id=1, source_target_pairs={{0,1},{1,2},{2,3},{3,4},{4,5},{5,6},{6,7},{7,0},{8,9},{9,10},{10,1... | collective-permute-start | bytes 1966088 | tf_op jit(solution)/shard_map/ppermute | solution.py:362
  57.1 11.8 %collective-permute-done.9.refs_6_ = bf16[256,1280]{1,0:T(8,128)(2,1)} collective-permute-done((bf16[256,1280]{1,0:T(8,128)(2,1)S(1)}, bf16[256,1280]{1,0:T(8,128)(2,1)}, u32[]{:S(2)}, u32[]{:S(2)}) %collective-permute-start.9) | collective-permute-done | bytes 655392 | tf_op jit(solution)/shard_map/ppermute | solution.py:362
  68.8 3.3 %collective-permute-start.11 = (bf16[256,1280]{1,0:T(8,128)(2,1)S(1)}, bf16[256,1280]{1,0:T(8,128)(2,1)}, u32[]{:S(2)}, u32[]{:S(2)}) collective-permute-start(bf16[256,1280]{1,0:T(8,128)(2,1)S(1)} %collective-permute-done.6.refs_10_), channel_id=1, source_target_pairs={{0,1},{1,2},{2,3},{3,4},{4,5},{5,6},{6,7},{7,0},{8,9},{9,10},{10,1... | collective-permute-start | bytes 1966088 | tf_op jit(solution)/shard_map/ppermute | solution.py:362
  72.2 7.2 %collective-permute-done.5.refs_3_ = bf16[256,1280]{1,0:T(8,128)(2,1)} collective-permute-done((bf16[256,1280]{1,0:T(8,128)(2,1)S(1)}, bf16[256,1280]{1,0:T(8,128)(2,1)}, u32[]{:S(2)}, u32[]{:S(2)}) %collective-permute-start.5) | collective-permute-done | bytes 655392 | tf_op jit(solution)/shard_map/ppermute | solution.py:362
  79.4 3.8 %collective-permute-start.8 = (bf16[256,1280]{1,0:T(8,128)(2,1)}, bf16[256,1280]{1,0:T(8,128)(2,1)}, u32[]{:S(2)}, u32[]{:S(2)}) collective-permute-start(bf16[256,1280]{1,0:T(8,128)(2,1)} %collective-permute-done.5.refs_3_), channel_id=1, source_target_pairs={{0,1},{1,2},{2,3},{3,4},{4,5},{5,6},{6,7},{7,0},{8,9},{9,10},{10,1... | collective-permute-start | bytes 1966088 | tf_op jit(solution)/shard_map/ppermute | solution.py:362
  83.2 4.6 %collective-permute-done.12.refs_14_ = bf16[256,1280]{1,0:T(8,128)(2,1)} collective-permute-done((bf16[256,1280]{1,0:T(8,128)(2,1)S(1)}, bf16[256,1280]{1,0:T(8,128)(2,1)}, u32[]{:S(2)}, u32[]{:S(2)}) %collective-permute-start.12) | collective-permute-done | bytes 655392 | tf_op jit(solution)/shard_map/ppermute | solution.py:362
  90.7 11.2 %collective-permute-done.10.refs_7_ = bf16[256,1280]{1,0:T(8,128)(2,1)} collective-permute-done((bf16[256,1280]{1,0:T(8,128)(2,1)}, bf16[256,1280]{1,0:T(8,128)(2,1)}, u32[]{:S(2)}, u32[]{:S(2)}) %collective-permute-start.10) | collective-permute-done | bytes 655392 | tf_op jit(solution)/shard_map/ppermute | solution.py:362
  101.9 5.0 %collective-permute-done.8.refs_4_ = bf16[256,1280]{1,0:T(8,128)(2,1)} collective-permute-done((bf16[256,1280]{1,0:T(8,128)(2,1)}, bf16[256,1280]{1,0:T(8,128)(2,1)}, u32[]{:S(2)}, u32[]{:S(2)}) %collective-permute-start.8) | collective-permute-done | bytes 655392 | tf_op jit(solution)/shard_map/ppermute | solution.py:362
  106.9 10.5 %gate_units.1.ready_ref.refs_0_ = bf16[1280,512]{1,0:T(8,128)(2,1)} custom-call(bf16[1280,2048]{1,0:T(8,128)(2,1)} %bitcast.4.rows_ref, bf16[256,1280]{1,0:T(8,128)(2,1)} %copy-done.5, bf16[256,1280]{1,0:T(8,128)(2,1)} %copy-done.9, bf16[256,1280]{1,0:T(8,128)(2,1)} %copy-done.12, bf16[256,1280]{1,0:T(8,128)(2,1)} %collective-permute-done.5.refs_3_, ...), custom_call_target="tpu_custom_call" | custom-call | flops 5368709120 | bytes 10747904 | tf_op jit(solution)/shard_map/gate_units/pallas_call | solution.py:204
  117.4 14.5 %front.1 = (bf16[1280,512]{1,0:T(8,128)(2,1)}, bf16[2304,512]{1,0:T(8,128)(2,1)}) custom-call(bf16[1280,2048]{1,0:T(8,128)(2,1)} %bitcast.4.rows_ref, bf16[1280,512]{1,0:T(8,128)(2,1)} %gate_units.1.ready_ref.refs_0_, bf16[256,1280]{1,0:T(8,128)(2,1)} %copy-done.5, bf16[256,1280]{1,0:T(8,128)(2,1)} %copy-done.9, bf16[256,1280]{1,0:T(8,128)(2,1)} %copy-done.12, ...), custom_call_target="tpu_custom_call" | custom-call | flops 8053063680 | bytes 12058624 | tf_op jit(solution)/shard_map/front/pallas_call | solution.py:261
  131.9 7.3 %all-to-all-start.2 = ((bf16[32,72,512]{2,1,0:T(8,128)(2,1)}), bf16[32,72,512]{2,1,0:T(8,128)(2,1)S(1)}, u32[]{:S(2)}, u32[]{:S(2)}) async-start(bf16[32,72,512]{2,1,0:T(8,128)(2,1)} %bitcast.23), calls=%async_computation.2 | async-start | bytes 4718592 | tf_op jit(solution)/shard_map/all_to_all | solution.py:441
  139.3 3.8 %collective-permute-start.14 = (bf16[128,512]{1,0:T(8,128)(2,1)S(1)}, bf16[128,512]{1,0:T(8,128)(2,1)S(1)}, u32[]{:S(2)}, u32[]{:S(2)}) collective-permute-start(bf16[128,512]{1,0:T(8,128)(2,1)S(1)} %get-tuple-element.42.refs_2_), channel_id=1, source_target_pairs={{0,1},{1,2},{2,3},{3,4},{4,5},{5,6},{6,7},{7,0},{8,9},{9,10},{10,1... | collective-permute-start | bytes 393224 | tf_op jit(solution)/shard_map/ppermute | solution.py:362
  146.3 4.3 %collective-permute-done.17.refs_14_ = bf16[128,512]{1,0:T(8,128)(2,1)S(1)} collective-permute-done((bf16[128,512]{1,0:T(8,128)(2,1)S(1)}, bf16[128,512]{1,0:T(8,128)(2,1)S(1)}, u32[]{:S(2)}, u32[]{:S(2)}) %collective-permute-start.17) | collective-permute-done | bytes 131104 | tf_op jit(solution)/shard_map/ppermute | solution.py:362
  170.0 3.7 %collective-permute-done.27.refs_17_ = bf16[128,512]{1,0:T(8,128)(2,1)S(1)} collective-permute-done((bf16[128,512]{1,0:T(8,128)(2,1)S(1)}, bf16[128,512]{1,0:T(8,128)(2,1)S(1)}, u32[]{:S(2)}, u32[]{:S(2)}) %collective-permute-start.27) | collective-permute-done | bytes 131104 | tf_op jit(solution)/shard_map/ppermute | solution.py:362
  174.4 7.5 %late_down_rows.1 = bf16[2304,512]{1,0:T(8,128)(2,1)} custom-call(bf16[1280,512]{1,0:T(8,128)(2,1)} %gate_units.1.ready_ref.refs_0_, bf16[1280,512]{1,0:T(8,128)(2,1)} %get-tuple-element.41.refs_1_, bf16[128,512]{1,0:T(8,128)(2,1)} %copy-done.8, bf16[128,512]{1,0:T(8,128)(2,1)} %copy-done.15, bf16[128,512]{1,0:T(8,128)(2,1)} %copy-done.19, ...), custom_call_target="tpu_custom_call" | custom-call | flops 2684354560 | bytes 7340032 | tf_op jit(solution)/shard_map/late_down_rows/pallas_call | solution.py:322
  181.9 7.1 %all-to-all-start.1 = ((bf16[32,72,512]{2,1,0:T(8,128)(2,1)}), bf16[32,72,512]{2,1,0:T(8,128)(2,1)}, u32[]{:S(2)}, u32[]{:S(2)}) async-start(bf16[32,72,512]{2,1,0:T(8,128)(2,1)} %bitcast.24), calls=%async_computation.1 | async-start | bytes 4718592 | tf_op jit(solution)/shard_map/all_to_all | solution.py:441
  192.0 30.0 %all-to-all-done.1 = bf16[32,72,512]{2,1,0:T(8,128)(2,1)} async-done(((bf16[32,72,512]{2,1,0:T(8,128)(2,1)}), bf16[32,72,512]{2,1,0:T(8,128)(2,1)}, u32[]{:S(2)}, u32[]{:S(2)}) %all-to-all-start.1) | async-done | bytes 2359328 | tf_op jit(solution)/shard_map/all_to_all | solution.py:441
  223.7 3.8 %mix.3 = bf16[128,2048]{1,0:T(8,128)(2,1)} custom-call(bf16[512,2304]{1,0:T(8,128)(2,1)S(1)} %copy-done.2, bf16[2304,512]{1,0:T(8,128)(2,1)} %bitcast.11.back_ref, bf16[128,1024]{1,0:T(8,128)(2,1)S(1)} %mix.2.refs_0_), custom_call_target="tpu_custom_call" | custom-call | flops 1207959552 | bytes 5242880 | tf_op jit(solution)/shard_map/mix/pallas_call | solution.py:132
  (110 shorter events, 42.5 us)
Async XLA Ops:
  3.2 19.0 %collective-permute-start = (bf16[256,1280]{1,0:T(8,128)(2,1)S(1)}, bf16[256,1280]{1,0:T(8,128)(2,1)S(1)}, u32[]{:S(2)}, u32[]{:S(2)}) collective-permute-start(bf16[256,1280]{1,0:T(8,128)(2,1)S(1)} %maximum_maximum_fusion.refs_0_), channel_id=1, source_target_pairs={{0,1},{1,2},{2,3},{3,4},{4,5},{5,6},{6,7},{7,0},{8,9},{9,10},{10,1... | collective-permute-start | bytes 1966088 | tf_op jit(solution)/shard_map/ppermute | solution.py:362
  6.4 18.9 %collective-permute-start.1 = (bf16[256,1280]{1,0:T(8,128)(2,1)S(1)}, bf16[256,1280]{1,0:T(8,128)(2,1)S(1)}, u32[]{:S(2)}, u32[]{:S(2)}) collective-permute-start(bf16[256,1280]{1,0:T(8,128)(2,1)S(1)} %maximum_maximum_fusion.refs_0_), channel_id=1, source_target_pairs={{0,7},{1,0},{2,1},{3,2},{4,3},{5,4},{6,5},{7,6},{8,15},{9,8},{10,9... | collective-permute-start | bytes 1966088 | tf_op jit(solution)/shard_map/ppermute | solution.py:362
  6.5 31.5 %collective-permute-start.4 = (bf16[256,1280]{1,0:T(8,128)(2,1)S(1)}, bf16[256,1280]{1,0:T(8,128)(2,1)}, u32[]{:S(2)}, u32[]{:S(2)}) collective-permute-start(bf16[256,1280]{1,0:T(8,128)(2,1)S(1)} %maximum_maximum_fusion.1.refs_8_), channel_id=1, source_target_pairs={{0,7},{1,0},{2,1},{3,2},{4,3},{5,4},{6,5},{7,6},{8,15},{9,8},{10,9... | collective-permute-start | bytes 1966088 | tf_op jit(solution)/shard_map/ppermute | solution.py:362
  11.3 79.4 %all-to-all-start = ((bf16[32,40,2048]{2,1,0:T(8,128)(2,1)}), bf16[32,40,2048]{2,1,0:T(8,128)(2,1)}, u32[]{:S(2)}, u32[]{:S(2)}) async-start(bf16[32,40,2048]{2,1,0:T(8,128)(2,1)} %bitcast.22), calls=%async_computation | async-start | bytes 10485760 | tf_op jit(solution)/shard_map/all_to_all | solution.py:416
  18.9 19.1 %collective-permute-start.3 = (bf16[256,1280]{1,0:T(8,128)(2,1)S(1)}, bf16[256,1280]{1,0:T(8,128)(2,1)S(1)}, u32[]{:S(2)}, u32[]{:S(2)}) collective-permute-start(bf16[256,1280]{1,0:T(8,128)(2,1)S(1)} %maximum_maximum_fusion.1.refs_8_), channel_id=1, source_target_pairs={{0,1},{1,2},{2,3},{3,4},{4,5},{5,6},{6,7},{7,0},{8,9},{9,10},{10,1... | collective-permute-start | bytes 1966088 | tf_op jit(solution)/shard_map/ppermute | solution.py:362
  22.2 29.1 %collective-permute-start.2 = (bf16[256,1280]{1,0:T(8,128)(2,1)S(1)}, bf16[256,1280]{1,0:T(8,128)(2,1)S(1)}, u32[]{:S(2)}, u32[]{:S(2)}) collective-permute-start(bf16[256,1280]{1,0:T(8,128)(2,1)S(1)} %collective-permute-done.refs_1_), channel_id=1, source_target_pairs={{0,1},{1,2},{2,3},{3,4},{4,5},{5,6},{6,7},{7,0},{8,9},{9,10},{10,1... | collective-permute-start | bytes 1966088 | tf_op jit(solution)/shard_map/ppermute | solution.py:362
  38.0 19.1 %collective-permute-start.7 = (bf16[256,1280]{1,0:T(8,128)(2,1)}, bf16[256,1280]{1,0:T(8,128)(2,1)S(1)}, u32[]{:S(2)}, u32[]{:S(2)}) collective-permute-start(bf16[256,1280]{1,0:T(8,128)(2,1)} %collective-permute-done.4.refs_12_), channel_id=1, source_target_pairs={{0,7},{1,0},{2,1},{3,2},{4,3},{5,4},{6,5},{7,6},{8,15},{9,8},{10,9... | collective-permute-start | bytes 1966088 | tf_op jit(solution)/shard_map/ppermute | solution.py:362
  38.0 30.9 %collective-permute-start.9 = (bf16[256,1280]{1,0:T(8,128)(2,1)S(1)}, bf16[256,1280]{1,0:T(8,128)(2,1)}, u32[]{:S(2)}, u32[]{:S(2)}) collective-permute-start(bf16[256,1280]{1,0:T(8,128)(2,1)S(1)} %collective-permute-done.1.refs_5_), channel_id=1, source_target_pairs={{0,7},{1,0},{2,1},{3,2},{4,3},{5,4},{6,5},{7,6},{8,15},{9,8},{10,9... | collective-permute-start | bytes 1966088 | tf_op jit(solution)/shard_map/ppermute | solution.py:362
  38.0 30.8 %collective-permute-start.6 = (bf16[256,1280]{1,0:T(8,128)(2,1)S(1)}, bf16[256,1280]{1,0:T(8,128)(2,1)S(1)}, u32[]{:S(2)}, u32[]{:S(2)}) collective-permute-start(bf16[256,1280]{1,0:T(8,128)(2,1)S(1)} %collective-permute-done.3.refs_9_), channel_id=1, source_target_pairs={{0,1},{1,2},{2,3},{3,4},{4,5},{5,6},{6,7},{7,0},{8,9},{9,10},{10,1... | collective-permute-start | bytes 1966088 | tf_op jit(solution)/shard_map/ppermute | solution.py:362
  51.3 28.1 %collective-permute-start.5 = (bf16[256,1280]{1,0:T(8,128)(2,1)S(1)}, bf16[256,1280]{1,0:T(8,128)(2,1)}, u32[]{:S(2)}, u32[]{:S(2)}) collective-permute-start(bf16[256,1280]{1,0:T(8,128)(2,1)S(1)} %collective-permute-done.2.refs_2_), channel_id=1, source_target_pairs={{0,1},{1,2},{2,3},{3,4},{4,5},{5,6},{6,7},{7,0},{8,9},{9,10},{10,1... | collective-permute-start | bytes 1966088 | tf_op jit(solution)/shard_map/ppermute | solution.py:362
  68.8 19.0 %collective-permute-start.12 = (bf16[256,1280]{1,0:T(8,128)(2,1)S(1)}, bf16[256,1280]{1,0:T(8,128)(2,1)}, u32[]{:S(2)}, u32[]{:S(2)}) collective-permute-start(bf16[256,1280]{1,0:T(8,128)(2,1)S(1)} %collective-permute-done.7.refs_13_), channel_id=1, source_target_pairs={{0,7},{1,0},{2,1},{3,2},{4,3},{5,4},{6,5},{7,6},{8,15},{9,8},{10,9... | collective-permute-start | bytes 1966088 | tf_op jit(solution)/shard_map/ppermute | solution.py:362
  68.8 33.0 %collective-permute-start.10 = (bf16[256,1280]{1,0:T(8,128)(2,1)}, bf16[256,1280]{1,0:T(8,128)(2,1)}, u32[]{:S(2)}, u32[]{:S(2)}) collective-permute-start(bf16[256,1280]{1,0:T(8,128)(2,1)} %collective-permute-done.9.refs_6_), channel_id=1, source_target_pairs={{0,7},{1,0},{2,1},{3,2},{4,3},{5,4},{6,5},{7,6},{8,15},{9,8},{10,9... | collective-permute-start | bytes 1966088 | tf_op jit(solution)/shard_map/ppermute | solution.py:362
  68.8 48.6 %collective-permute-start.11 = (bf16[256,1280]{1,0:T(8,128)(2,1)S(1)}, bf16[256,1280]{1,0:T(8,128)(2,1)}, u32[]{:S(2)}, u32[]{:S(2)}) collective-permute-start(bf16[256,1280]{1,0:T(8,128)(2,1)S(1)} %collective-permute-done.6.refs_10_), channel_id=1, source_target_pairs={{0,1},{1,2},{2,3},{3,4},{4,5},{5,6},{6,7},{7,0},{8,9},{9,10},{10,1... | collective-permute-start | bytes 1966088 | tf_op jit(solution)/shard_map/ppermute | solution.py:362
  79.4 27.5 %collective-permute-start.8 = (bf16[256,1280]{1,0:T(8,128)(2,1)}, bf16[256,1280]{1,0:T(8,128)(2,1)}, u32[]{:S(2)}, u32[]{:S(2)}) collective-permute-start(bf16[256,1280]{1,0:T(8,128)(2,1)} %collective-permute-done.5.refs_3_), channel_id=1, source_target_pairs={{0,1},{1,2},{2,3},{3,4},{4,5},{5,6},{6,7},{7,0},{8,9},{9,10},{10,1... | collective-permute-start | bytes 1966088 | tf_op jit(solution)/shard_map/ppermute | solution.py:362
  87.8 29.6 %collective-permute-start.13 = (bf16[256,1280]{1,0:T(8,128)(2,1)}, bf16[256,1280]{1,0:T(8,128)(2,1)}, u32[]{:S(2)}, u32[]{:S(2)}) collective-permute-start(bf16[256,1280]{1,0:T(8,128)(2,1)} %collective-permute-done.12.refs_14_), channel_id=1, source_target_pairs={{0,7},{1,0},{2,1},{3,2},{4,3},{5,4},{6,5},{7,6},{8,15},{9,8},{10,9... | collective-permute-start | bytes 1966088 | tf_op jit(solution)/shard_map/ppermute | solution.py:362
  131.9 50.0 %all-to-all-start.2 = ((bf16[32,72,512]{2,1,0:T(8,128)(2,1)}), bf16[32,72,512]{2,1,0:T(8,128)(2,1)S(1)}, u32[]{:S(2)}, u32[]{:S(2)}) async-start(bf16[32,72,512]{2,1,0:T(8,128)(2,1)} %bitcast.23), calls=%async_computation.2 | async-start | bytes 4718592 | tf_op jit(solution)/shard_map/all_to_all | solution.py:441
  143.0 7.6 %collective-permute-start.17 = (bf16[128,512]{1,0:T(8,128)(2,1)S(1)}, bf16[128,512]{1,0:T(8,128)(2,1)S(1)}, u32[]{:S(2)}, u32[]{:S(2)}) collective-permute-start(bf16[128,512]{1,0:T(8,128)(2,1)S(1)} %get-tuple-element.44.refs_10_), channel_id=1, source_target_pairs={{0,7},{1,0},{2,1},{3,2},{4,3},{5,4},{6,5},{7,6},{8,15},{9,8},{10,9... | collective-permute-start | bytes 393224 | tf_op jit(solution)/shard_map/ppermute | solution.py:362
  143.0 9.4 %collective-permute-start.19 = (bf16[128,512]{1,0:T(8,128)(2,1)S(1)}, bf16[128,512]{1,0:T(8,128)(2,1)S(1)}, u32[]{:S(2)}, u32[]{:S(2)}) collective-permute-start(bf16[128,512]{1,0:T(8,128)(2,1)S(1)} %get-tuple-element.42.refs_2_), channel_id=1, source_target_pairs={{0,7},{1,0},{2,1},{3,2},{4,3},{5,4},{6,5},{7,6},{8,15},{9,8},{10,9... | collective-permute-start | bytes 393224 | tf_op jit(solution)/shard_map/ppermute | solution.py:362
  143.0 11.5 %collective-permute-start.16 = (bf16[128,512]{1,0:T(8,128)(2,1)S(1)}, bf16[128,512]{1,0:T(8,128)(2,1)S(1)}, u32[]{:S(2)}, u32[]{:S(2)}) collective-permute-start(bf16[128,512]{1,0:T(8,128)(2,1)S(1)} %get-tuple-element.44.refs_10_), channel_id=1, source_target_pairs={{0,1},{1,2},{2,3},{3,4},{4,5},{5,6},{6,7},{7,0},{8,9},{9,10},{10,1... | collective-permute-start | bytes 393224 | tf_op jit(solution)/shard_map/ppermute | solution.py:362
  152.4 7.2 %collective-permute-start.21 = (bf16[128,512]{1,0:T(8,128)(2,1)S(1)}, bf16[128,512]{1,0:T(8,128)(2,1)S(1)}, u32[]{:S(2)}, u32[]{:S(2)}) collective-permute-start(bf16[128,512]{1,0:T(8,128)(2,1)S(1)} %collective-permute-done.17.refs_14_), channel_id=1, source_target_pairs={{0,7},{1,0},{2,1},{3,2},{4,3},{5,4},{6,5},{7,6},{8,15},{9,8},{10,9... | collective-permute-start | bytes 393224 | tf_op jit(solution)/shard_map/ppermute | solution.py:362
  154.5 7.3 %collective-permute-start.20 = (bf16[128,512]{1,0:T(8,128)(2,1)S(1)}, bf16[128,512]{1,0:T(8,128)(2,1)S(1)}, u32[]{:S(2)}, u32[]{:S(2)}) collective-permute-start(bf16[128,512]{1,0:T(8,128)(2,1)S(1)} %collective-permute-done.16.refs_11_), channel_id=1, source_target_pairs={{0,1},{1,2},{2,3},{3,4},{4,5},{5,6},{6,7},{7,0},{8,9},{9,10},{10,1... | collective-permute-start | bytes 393224 | tf_op jit(solution)/shard_map/ppermute | solution.py:362
  161.6 7.6 %collective-permute-start.24 = (bf16[128,512]{1,0:T(8,128)(2,1)S(1)}, bf16[128,512]{1,0:T(8,128)(2,1)S(1)}, u32[]{:S(2)}, u32[]{:S(2)}) collective-permute-start(bf16[128,512]{1,0:T(8,128)(2,1)S(1)} %collective-permute-done.23.refs_8_), channel_id=1, source_target_pairs={{0,7},{1,0},{2,1},{3,2},{4,3},{5,4},{6,5},{7,6},{8,15},{9,8},{10,9... | collective-permute-start | bytes 393224 | tf_op jit(solution)/shard_map/ppermute | solution.py:362
  161.8 7.3 %collective-permute-start.25 = (bf16[128,512]{1,0:T(8,128)(2,1)S(1)}, bf16[128,512]{1,0:T(8,128)(2,1)S(1)}, u32[]{:S(2)}, u32[]{:S(2)}) collective-permute-start(bf16[128,512]{1,0:T(8,128)(2,1)S(1)} %collective-permute-done.20.refs_12_), channel_id=1, source_target_pairs={{0,1},{1,2},{2,3},{3,4},{4,5},{5,6},{6,7},{7,0},{8,9},{9,10},{10,1... | collective-permute-start | bytes 393224 | tf_op jit(solution)/shard_map/ppermute | solution.py:362
  181.9 40.2 %all-to-all-start.1 = ((bf16[32,72,512]{2,1,0:T(8,128)(2,1)}), bf16[32,72,512]{2,1,0:T(8,128)(2,1)}, u32[]{:S(2)}, u32[]{:S(2)}) async-start(bf16[32,72,512]{2,1,0:T(8,128)(2,1)} %bitcast.24), calls=%async_computation.1 | async-start | bytes 4718592 | tf_op jit(solution)/shard_map/all_to_all | solution.py:441
  (36 other events, 734.3 us)

commit v3 on v2

--- a/solution.py
+++ b/solution.py
@@ -13,9 +13,9 @@
 PACKED = 72
 NONE = 200.0
 EARLY = 1024
-WINDOW = 3
+WINDOW = 2
 MIXER_FLOPS = 40 * 10**9
-ORDER = ("ABABABA", "ABABABB")
+ORDER = ("ABABAAB", "ABABABB")
 LATE_ORDER = ("efefefe", "efefeff")
 VMEM_LIMIT = 56 << 20
 

time: 228 us -> 218 us (0.956)
  starting transfers between devices: 61.9 us -> 52.2 us
    ppermute x28, starting transfers between devices: 39.9 us -> 29.9 us  [hop(): chain.append(lax.ppermute(piece, 'rep', pairs))]
    unnamed x58 -> x60, local copies, waits for them, and re-layouts: 5.47 us -> 5.46 us
  transfers between devices with their start and end apart: 31 -> 31, of which waited for: 20 -> 23; matrix products, arithmetic and copies ran while one was open for 0% -> 0% of each run, Pallas kernels for 11% -> 12%
where the time goes in v3:
time: 218 us
  waiting for transfers between devices  113 us (52%)
  starting transfers between devices  52.2 us (24%)
  Pallas kernels  43.5 us (20%)
  local copies, waits for them, and re-layouts  5.58 us (3%)
  other arithmetic  3.11 us (1%)
    ppermute x28, waiting for transfers between devices, hop(): chain.append(lax.ppermute(piece, 'rep', pairs))  82.9 us
    all_to_all x2, waiting for transfers between devices, per_device(): lax.all_to_all(sent.reshape(groups, PACKED, half), 'tok', split_axis=0, c...  30 us
    ppermute x28, starting transfers between devices, hop(): chain.append(lax.ppermute(piece, 'rep', pairs))  29.9 us
    all_to_all x2, starting transfers between devices, per_device(): lax.all_to_all(sent.reshape(groups, PACKED, half), 'tok', split_axis=0, c...  14.8 us
    pallas_call x1, Pallas kernels, front(): pl.pallas_call(functools.partial(front_kernel, ranks, rightwards), out_sh...  14.5 us
    pallas_call x1, Pallas kernels, gate_units(): pl.pallas_call(functools.partial(gate_kernel, len(pieces), rightward), ou...  10.5 us
    all_to_all x1, starting transfers between devices, per_device(): lax.all_to_all(send.reshape(groups, PAD, width), 'tok', split_axis=0, con...  7.58 us
    pallas_call x1, Pallas kernels, late_down_rows(): pl.pallas_call(functools.partial(late_down_kernel, len(units), pieces, ri...  7.5 us
  transfers between devices with their start and end apart: 31, of which 23 were waited for; matrix products, arithmetic and copies ran while one was open for 0% of the time, Pallas kernels for 12%

profile of v3, /device:TPU:96, one launch (start us, length us, event | category | flops | bytes accessed | tf_op | source)
XLA Modules:
  0.0 217.7 jit_solution(10457488767747431309)
XLA Ops:
  3.2 3.2 %collective-permute-start = (bf16[256,1280]{1,0:T(8,128)(2,1)S(1)}, bf16[256,1280]{1,0:T(8,128)(2,1)S(1)}, u32[]{:S(2)}, u32[]{:S(2)}) collective-permute-start(bf16[256,1280]{1,0:T(8,128)(2,1)S(1)} %maximum_maximum_fusion.refs_0_), channel_id=1, source_target_pairs={{0,1},{1,2},{2,3},{3,4},{4,5},{5,6},{6,7},{7,0},{8,9},{9,10},{10,1... | collective-permute-start | bytes 1966088 | tf_op jit(solution)/shard_map/ppermute | solution.py:362
  6.5 3.3 %collective-permute-start.5 = (bf16[256,1280]{1,0:T(8,128)(2,1)S(1)}, bf16[256,1280]{1,0:T(8,128)(2,1)}, u32[]{:S(2)}, u32[]{:S(2)}) collective-permute-start(bf16[256,1280]{1,0:T(8,128)(2,1)S(1)} %maximum_maximum_fusion.1.refs_8_), channel_id=1, source_target_pairs={{0,1},{1,2},{2,3},{3,4},{4,5},{5,6},{6,7},{7,0},{8,9},{9,10},{10,1... | collective-permute-start | bytes 1966088 | tf_op jit(solution)/shard_map/ppermute | solution.py:362
  9.8 4.5 %dispatch.1 = bf16[1280,2048]{1,0:T(8,128)(2,1)} custom-call(s32[8,128]{1,0:T(8,128)} %bitcast.19, bf16[128,2048]{1,0:T(8,128)(2,1)} %bitcast.25), custom_call_target="tpu_custom_call" | custom-call | flops 671088640 | bytes 5767168 | tf_op jit(solution)/shard_map/dispatch/pallas_call | solution.py:52
  14.4 7.6 %all-to-all-start = ((bf16[32,40,2048]{2,1,0:T(8,128)(2,1)}), bf16[32,40,2048]{2,1,0:T(8,128)(2,1)}, u32[]{:S(2)}, u32[]{:S(2)}) async-start(bf16[32,40,2048]{2,1,0:T(8,128)(2,1)} %bitcast.22), calls=%async_computation | async-start | bytes 10485760 | tf_op jit(solution)/shard_map/all_to_all | solution.py:416
  22.0 3.3 %collective-permute-done.1.refs_5_ = bf16[256,1280]{1,0:T(8,128)(2,1)S(1)} collective-permute-done((bf16[256,1280]{1,0:T(8,128)(2,1)S(1)}, bf16[256,1280]{1,0:T(8,128)(2,1)S(1)}, u32[]{:S(2)}, u32[]{:S(2)}) %collective-permute-start.1) | collective-permute-done | bytes 655392 | tf_op jit(solution)/shard_map/ppermute | solution.py:362
  27.3 8.3 %collective-permute-done.5.refs_9_ = bf16[256,1280]{1,0:T(8,128)(2,1)} collective-permute-done((bf16[256,1280]{1,0:T(8,128)(2,1)S(1)}, bf16[256,1280]{1,0:T(8,128)(2,1)}, u32[]{:S(2)}, u32[]{:S(2)}) %collective-permute-start.5) | collective-permute-done | bytes 655392 | tf_op jit(solution)/shard_map/ppermute | solution.py:362
  35.6 3.8 %collective-permute-done.6.refs_12_ = bf16[256,1280]{1,0:T(8,128)(2,1)} collective-permute-done((bf16[256,1280]{1,0:T(8,128)(2,1)S(1)}, bf16[256,1280]{1,0:T(8,128)(2,1)}, u32[]{:S(2)}, u32[]{:S(2)}) %collective-permute-start.6) | collective-permute-done | bytes 655392 | tf_op jit(solution)/shard_map/ppermute | solution.py:362
  41.5 8.2 %collective-permute-done.2.refs_2_ = bf16[256,1280]{1,0:T(8,128)(2,1)S(1)} collective-permute-done((bf16[256,1280]{1,0:T(8,128)(2,1)S(1)}, bf16[256,1280]{1,0:T(8,128)(2,1)S(1)}, u32[]{:S(2)}, u32[]{:S(2)}) %collective-permute-start.2) | collective-permute-done | bytes 655392 | tf_op jit(solution)/shard_map/ppermute | solution.py:362
  49.6 3.7 %collective-permute-done.3.refs_6_ = bf16[256,1280]{1,0:T(8,128)(2,1)S(1)} collective-permute-done((bf16[256,1280]{1,0:T(8,128)(2,1)S(1)}, bf16[256,1280]{1,0:T(8,128)(2,1)S(1)}, u32[]{:S(2)}, u32[]{:S(2)}) %collective-permute-start.3) | collective-permute-done | bytes 655392 | tf_op jit(solution)/shard_map/ppermute | solution.py:362
  55.4 8.4 %collective-permute-done.7.refs_10_ = bf16[256,1280]{1,0:T(8,128)(2,1)S(1)} collective-permute-done((bf16[256,1280]{1,0:T(8,128)(2,1)}, bf16[256,1280]{1,0:T(8,128)(2,1)S(1)}, u32[]{:S(2)}, u32[]{:S(2)}) %collective-permute-start.7) | collective-permute-done | bytes 655392 | tf_op jit(solution)/shard_map/ppermute | solution.py:362
  63.8 3.6 %collective-permute-done.8.refs_13_ = bf16[256,1280]{1,0:T(8,128)(2,1)S(1)} collective-permute-done((bf16[256,1280]{1,0:T(8,128)(2,1)}, bf16[256,1280]{1,0:T(8,128)(2,1)S(1)}, u32[]{:S(2)}, u32[]{:S(2)}) %collective-permute-start.8) | collective-permute-done | bytes 655392 | tf_op jit(solution)/shard_map/ppermute | solution.py:362
  67.4 9.2 %collective-permute-done.4.refs_3_ = bf16[256,1280]{1,0:T(8,128)(2,1)} collective-permute-done((bf16[256,1280]{1,0:T(8,128)(2,1)S(1)}, bf16[256,1280]{1,0:T(8,128)(2,1)}, u32[]{:S(2)}, u32[]{:S(2)}) %collective-permute-start.4) | collective-permute-done | bytes 655392 | tf_op jit(solution)/shard_map/ppermute | solution.py:362
  76.6 3.8 %collective-permute-start.9 = (bf16[256,1280]{1,0:T(8,128)(2,1)}, bf16[256,1280]{1,0:T(8,128)(2,1)}, u32[]{:S(2)}, u32[]{:S(2)}) collective-permute-start(bf16[256,1280]{1,0:T(8,128)(2,1)} %collective-permute-done.4.refs_3_), channel_id=1, source_target_pairs={{0,1},{1,2},{2,3},{3,4},{4,5},{5,6},{6,7},{7,0},{8,9},{9,10},{10,1... | collective-permute-start | bytes 1966088 | tf_op jit(solution)/shard_map/ppermute | solution.py:362
  81.5 12.7 %collective-permute-done.12.refs_14_ = bf16[256,1280]{1,0:T(8,128)(2,1)} collective-permute-done((bf16[256,1280]{1,0:T(8,128)(2,1)S(1)}, bf16[256,1280]{1,0:T(8,128)(2,1)}, u32[]{:S(2)}, u32[]{:S(2)}) %collective-permute-start.12) | collective-permute-done | bytes 655392 | tf_op jit(solution)/shard_map/ppermute | solution.py:362
  97.0 10.5 %gate_units.1.ready_ref.refs_0_ = bf16[1280,512]{1,0:T(8,128)(2,1)} custom-call(bf16[1280,2048]{1,0:T(8,128)(2,1)} %bitcast.4.rows_ref, bf16[256,1280]{1,0:T(8,128)(2,1)} %copy-done.5, bf16[256,1280]{1,0:T(8,128)(2,1)} %copy-done.9, bf16[256,1280]{1,0:T(8,128)(2,1)} %copy-done.11, bf16[256,1280]{1,0:T(8,128)(2,1)} %collective-permute-done.4.refs_3_, ...), custom_call_target="tpu_custom_call" | custom-call | flops 5368709120 | bytes 10747904 | tf_op jit(solution)/shard_map/gate_units/pallas_call | solution.py:204
  107.8 3.2 %collective-permute-done.13.refs_15_ = bf16[256,1280]{1,0:T(8,128)(2,1)} collective-permute-done((bf16[256,1280]{1,0:T(8,128)(2,1)}, bf16[256,1280]{1,0:T(8,128)(2,1)}, u32[]{:S(2)}, u32[]{:S(2)}) %collective-permute-start.13) | collective-permute-done | bytes 655392 | tf_op jit(solution)/shard_map/ppermute | solution.py:362
  111.0 14.5 %front.1 = (bf16[1280,512]{1,0:T(8,128)(2,1)}, bf16[2304,512]{1,0:T(8,128)(2,1)}) custom-call(bf16[1280,2048]{1,0:T(8,128)(2,1)} %bitcast.4.rows_ref, bf16[1280,512]{1,0:T(8,128)(2,1)} %gate_units.1.ready_ref.refs_0_, bf16[256,1280]{1,0:T(8,128)(2,1)} %copy-done.5, bf16[256,1280]{1,0:T(8,128)(2,1)} %copy-done.9, bf16[256,1280]{1,0:T(8,128)(2,1)} %copy-done.11, ...), custom_call_target="tpu_custom_call" | custom-call | flops 8053063680 | bytes 12058624 | tf_op jit(solution)/shard_map/front/pallas_call | solution.py:261
  125.4 7.3 %all-to-all-start.2 = ((bf16[32,72,512]{2,1,0:T(8,128)(2,1)}), bf16[32,72,512]{2,1,0:T(8,128)(2,1)S(1)}, u32[]{:S(2)}, u32[]{:S(2)}) async-start(bf16[32,72,512]{2,1,0:T(8,128)(2,1)} %bitcast.23), calls=%async_computation.2 | async-start | bytes 4718592 | tf_op jit(solution)/shard_map/all_to_all | solution.py:441
  151.2 3.2 %collective-permute-start.25 = (bf16[128,512]{1,0:T(8,128)(2,1)S(1)}, bf16[128,512]{1,0:T(8,128)(2,1)S(1)}, u32[]{:S(2)}, u32[]{:S(2)}) collective-permute-start(bf16[128,512]{1,0:T(8,128)(2,1)S(1)} %collective-permute-done.23.refs_12_), channel_id=1, source_target_pairs={{0,1},{1,2},{2,3},{3,4},{4,5},{5,6},{6,7},{7,0},{8,9},{9,10},{10,1... | collective-permute-start | bytes 393224 | tf_op jit(solution)/shard_map/ppermute | solution.py:362
  159.7 3.8 %collective-permute-done.27.refs_17_ = bf16[128,512]{1,0:T(8,128)(2,1)S(1)} collective-permute-done((bf16[128,512]{1,0:T(8,128)(2,1)S(1)}, bf16[128,512]{1,0:T(8,128)(2,1)S(1)}, u32[]{:S(2)}, u32[]{:S(2)}) %collective-permute-start.27) | collective-permute-done | bytes 131104 | tf_op jit(solution)/shard_map/ppermute | solution.py:362
  164.2 7.5 %late_down_rows.1 = bf16[2304,512]{1,0:T(8,128)(2,1)} custom-call(bf16[1280,512]{1,0:T(8,128)(2,1)} %gate_units.1.ready_ref.refs_0_, bf16[1280,512]{1,0:T(8,128)(2,1)} %get-tuple-element.45.refs_1_, bf16[128,512]{1,0:T(8,128)(2,1)} %copy-done.8, bf16[128,512]{1,0:T(8,128)(2,1)} %copy-done.16, bf16[128,512]{1,0:T(8,128)(2,1)} %copy-done.20, ...), custom_call_target="tpu_custom_call" | custom-call | flops 2684354560 | bytes 7340032 | tf_op jit(solution)/shard_map/late_down_rows/pallas_call | solution.py:322
  171.7 7.4 %all-to-all-start.1 = ((bf16[32,72,512]{2,1,0:T(8,128)(2,1)}), bf16[32,72,512]{2,1,0:T(8,128)(2,1)}, u32[]{:S(2)}, u32[]{:S(2)}) async-start(bf16[32,72,512]{2,1,0:T(8,128)(2,1)} %bitcast.24), calls=%async_computation.1 | async-start | bytes 4718592 | tf_op jit(solution)/shard_map/all_to_all | solution.py:441
  182.2 30.0 %all-to-all-done.1 = bf16[32,72,512]{2,1,0:T(8,128)(2,1)} async-done(((bf16[32,72,512]{2,1,0:T(8,128)(2,1)}), bf16[32,72,512]{2,1,0:T(8,128)(2,1)}, u32[]{:S(2)}, u32[]{:S(2)}) %all-to-all-start.1) | async-done | bytes 2359328 | tf_op jit(solution)/shard_map/all_to_all | solution.py:441
  213.9 3.8 %mix.3 = bf16[128,2048]{1,0:T(8,128)(2,1)} custom-call(bf16[512,2304]{1,0:T(8,128)(2,1)S(1)} %copy-done.2, bf16[2304,512]{1,0:T(8,128)(2,1)} %bitcast.11.back_ref, bf16[128,1024]{1,0:T(8,128)(2,1)S(1)} %mix.2.refs_0_), custom_call_target="tpu_custom_call" | custom-call | flops 1207959552 | bytes 5242880 | tf_op jit(solution)/shard_map/mix/pallas_call | solution.py:132
  (112 shorter events, 42.3 us)
Async XLA Ops:
  3.2 18.7 %collective-permute-start = (bf16[256,1280]{1,0:T(8,128)(2,1)S(1)}, bf16[256,1280]{1,0:T(8,128)(2,1)S(1)}, u32[]{:S(2)}, u32[]{:S(2)}) collective-permute-start(bf16[256,1280]{1,0:T(8,128)(2,1)S(1)} %maximum_maximum_fusion.refs_0_), channel_id=1, source_target_pairs={{0,1},{1,2},{2,3},{3,4},{4,5},{5,6},{6,7},{7,0},{8,9},{9,10},{10,1... | collective-permute-start | bytes 1966088 | tf_op jit(solution)/shard_map/ppermute | solution.py:362
  6.4 18.9 %collective-permute-start.1 = (bf16[256,1280]{1,0:T(8,128)(2,1)S(1)}, bf16[256,1280]{1,0:T(8,128)(2,1)S(1)}, u32[]{:S(2)}, u32[]{:S(2)}) collective-permute-start(bf16[256,1280]{1,0:T(8,128)(2,1)S(1)} %maximum_maximum_fusion.refs_0_), channel_id=1, source_target_pairs={{0,7},{1,0},{2,1},{3,2},{4,3},{5,4},{6,5},{7,6},{8,15},{9,8},{10,9... | collective-permute-start | bytes 1966088 | tf_op jit(solution)/shard_map/ppermute | solution.py:362
  6.5 29.1 %collective-permute-start.5 = (bf16[256,1280]{1,0:T(8,128)(2,1)S(1)}, bf16[256,1280]{1,0:T(8,128)(2,1)}, u32[]{:S(2)}, u32[]{:S(2)}) collective-permute-start(bf16[256,1280]{1,0:T(8,128)(2,1)S(1)} %maximum_maximum_fusion.1.refs_8_), channel_id=1, source_target_pairs={{0,1},{1,2},{2,3},{3,4},{4,5},{5,6},{6,7},{7,0},{8,9},{9,10},{10,1... | collective-permute-start | bytes 1966088 | tf_op jit(solution)/shard_map/ppermute | solution.py:362
  9.8 29.6 %collective-permute-start.6 = (bf16[256,1280]{1,0:T(8,128)(2,1)S(1)}, bf16[256,1280]{1,0:T(8,128)(2,1)}, u32[]{:S(2)}, u32[]{:S(2)}) collective-permute-start(bf16[256,1280]{1,0:T(8,128)(2,1)S(1)} %maximum_maximum_fusion.1.refs_8_), channel_id=1, source_target_pairs={{0,7},{1,0},{2,1},{3,2},{4,3},{5,4},{6,5},{7,6},{8,15},{9,8},{10,9... | collective-permute-start | bytes 1966088 | tf_op jit(solution)/shard_map/ppermute | solution.py:362
  14.4 82.7 %all-to-all-start = ((bf16[32,40,2048]{2,1,0:T(8,128)(2,1)}), bf16[32,40,2048]{2,1,0:T(8,128)(2,1)}, u32[]{:S(2)}, u32[]{:S(2)}) async-start(bf16[32,40,2048]{2,1,0:T(8,128)(2,1)} %bitcast.22), calls=%async_computation | async-start | bytes 10485760 | tf_op jit(solution)/shard_map/all_to_all | solution.py:416
  25.3 24.4 %collective-permute-start.2 = (bf16[256,1280]{1,0:T(8,128)(2,1)S(1)}, bf16[256,1280]{1,0:T(8,128)(2,1)S(1)}, u32[]{:S(2)}, u32[]{:S(2)}) collective-permute-start(bf16[256,1280]{1,0:T(8,128)(2,1)S(1)} %collective-permute-done.refs_1_), channel_id=1, source_target_pairs={{0,1},{1,2},{2,3},{3,4},{4,5},{5,6},{6,7},{7,0},{8,9},{9,10},{10,1... | collective-permute-start | bytes 1966088 | tf_op jit(solution)/shard_map/ppermute | solution.py:362
  25.3 28.0 %collective-permute-start.3 = (bf16[256,1280]{1,0:T(8,128)(2,1)S(1)}, bf16[256,1280]{1,0:T(8,128)(2,1)S(1)}, u32[]{:S(2)}, u32[]{:S(2)}) collective-permute-start(bf16[256,1280]{1,0:T(8,128)(2,1)S(1)} %collective-permute-done.1.refs_5_), channel_id=1, source_target_pairs={{0,7},{1,0},{2,1},{3,2},{4,3},{5,4},{6,5},{7,6},{8,15},{9,8},{10,9... | collective-permute-start | bytes 1966088 | tf_op jit(solution)/shard_map/ppermute | solution.py:362
  39.4 24.4 %collective-permute-start.7 = (bf16[256,1280]{1,0:T(8,128)(2,1)}, bf16[256,1280]{1,0:T(8,128)(2,1)S(1)}, u32[]{:S(2)}, u32[]{:S(2)}) collective-permute-start(bf16[256,1280]{1,0:T(8,128)(2,1)} %collective-permute-done.5.refs_9_), channel_id=1, source_target_pairs={{0,1},{1,2},{2,3},{3,4},{4,5},{5,6},{6,7},{7,0},{8,9},{9,10},{10,1... | collective-permute-start | bytes 1966088 | tf_op jit(solution)/shard_map/ppermute | solution.py:362
  39.4 28.0 %collective-permute-start.8 = (bf16[256,1280]{1,0:T(8,128)(2,1)}, bf16[256,1280]{1,0:T(8,128)(2,1)S(1)}, u32[]{:S(2)}, u32[]{:S(2)}) collective-permute-start(bf16[256,1280]{1,0:T(8,128)(2,1)} %collective-permute-done.6.refs_12_), channel_id=1, source_target_pairs={{0,7},{1,0},{2,1},{3,2},{4,3},{5,4},{6,5},{7,6},{8,15},{9,8},{10,9... | collective-permute-start | bytes 1966088 | tf_op jit(solution)/shard_map/ppermute | solution.py:362
  53.4 23.2 %collective-permute-start.4 = (bf16[256,1280]{1,0:T(8,128)(2,1)S(1)}, bf16[256,1280]{1,0:T(8,128)(2,1)}, u32[]{:S(2)}, u32[]{:S(2)}) collective-permute-start(bf16[256,1280]{1,0:T(8,128)(2,1)S(1)} %collective-permute-done.2.refs_2_), channel_id=1, source_target_pairs={{0,1},{1,2},{2,3},{3,4},{4,5},{5,6},{6,7},{7,0},{8,9},{9,10},{10,1... | collective-permute-start | bytes 1966088 | tf_op jit(solution)/shard_map/ppermute | solution.py:362
  53.4 28.0 %collective-permute-start.10 = (bf16[256,1280]{1,0:T(8,128)(2,1)S(1)}, bf16[256,1280]{1,0:T(8,128)(2,1)S(1)}, u32[]{:S(2)}, u32[]{:S(2)}) collective-permute-start(bf16[256,1280]{1,0:T(8,128)(2,1)S(1)} %collective-permute-done.3.refs_6_), channel_id=1, source_target_pairs={{0,7},{1,0},{2,1},{3,2},{4,3},{5,4},{6,5},{7,6},{8,15},{9,8},{10,9... | collective-permute-start | bytes 1966088 | tf_op jit(solution)/shard_map/ppermute | solution.py:362
  67.4 26.7 %collective-permute-start.12 = (bf16[256,1280]{1,0:T(8,128)(2,1)S(1)}, bf16[256,1280]{1,0:T(8,128)(2,1)}, u32[]{:S(2)}, u32[]{:S(2)}) collective-permute-start(bf16[256,1280]{1,0:T(8,128)(2,1)S(1)} %collective-permute-done.8.refs_13_), channel_id=1, source_target_pairs={{0,7},{1,0},{2,1},{3,2},{4,3},{5,4},{6,5},{7,6},{8,15},{9,8},{10,9... | collective-permute-start | bytes 1966088 | tf_op jit(solution)/shard_map/ppermute | solution.py:362
  76.6 20.4 %collective-permute-start.9 = (bf16[256,1280]{1,0:T(8,128)(2,1)}, bf16[256,1280]{1,0:T(8,128)(2,1)}, u32[]{:S(2)}, u32[]{:S(2)}) collective-permute-start(bf16[256,1280]{1,0:T(8,128)(2,1)} %collective-permute-done.4.refs_3_), channel_id=1, source_target_pairs={{0,1},{1,2},{2,3},{3,4},{4,5},{5,6},{6,7},{7,0},{8,9},{9,10},{10,1... | collective-permute-start | bytes 1966088 | tf_op jit(solution)/shard_map/ppermute | solution.py:362
  81.5 26.3 %collective-permute-start.11 = (bf16[256,1280]{1,0:T(8,128)(2,1)S(1)}, bf16[256,1280]{1,0:T(8,128)(2,1)}, u32[]{:S(2)}, u32[]{:S(2)}) collective-permute-start(bf16[256,1280]{1,0:T(8,128)(2,1)S(1)} %collective-permute-done.7.refs_10_), channel_id=1, source_target_pairs={{0,1},{1,2},{2,3},{3,4},{4,5},{5,6},{6,7},{7,0},{8,9},{9,10},{10,1... | collective-permute-start | bytes 1966088 | tf_op jit(solution)/shard_map/ppermute | solution.py:362
  94.1 16.8 %collective-permute-start.13 = (bf16[256,1280]{1,0:T(8,128)(2,1)}, bf16[256,1280]{1,0:T(8,128)(2,1)}, u32[]{:S(2)}, u32[]{:S(2)}) collective-permute-start(bf16[256,1280]{1,0:T(8,128)(2,1)} %collective-permute-done.12.refs_14_), channel_id=1, source_target_pairs={{0,7},{1,0},{2,1},{3,2},{4,3},{5,4},{6,5},{7,6},{8,15},{9,8},{10,9... | collective-permute-start | bytes 1966088 | tf_op jit(solution)/shard_map/ppermute | solution.py:362
  125.4 46.3 %all-to-all-start.2 = ((bf16[32,72,512]{2,1,0:T(8,128)(2,1)}), bf16[32,72,512]{2,1,0:T(8,128)(2,1)S(1)}, u32[]{:S(2)}, u32[]{:S(2)}) async-start(bf16[32,72,512]{2,1,0:T(8,128)(2,1)} %bitcast.23), calls=%async_computation.2 | async-start | bytes 4718592 | tf_op jit(solution)/shard_map/all_to_all | solution.py:441
  132.8 6.4 %collective-permute-start.14 = (bf16[128,512]{1,0:T(8,128)(2,1)S(1)}, bf16[128,512]{1,0:T(8,128)(2,1)S(1)}, u32[]{:S(2)}, u32[]{:S(2)}) collective-permute-start(bf16[128,512]{1,0:T(8,128)(2,1)S(1)} %get-tuple-element.46.refs_2_), channel_id=1, source_target_pairs={{0,1},{1,2},{2,3},{3,4},{4,5},{5,6},{6,7},{7,0},{8,9},{9,10},{10,1... | collective-permute-start | bytes 393224 | tf_op jit(solution)/shard_map/ppermute | solution.py:362
  133.5 6.7 %collective-permute-start.15 = (bf16[128,512]{1,0:T(8,128)(2,1)S(1)}, bf16[128,512]{1,0:T(8,128)(2,1)S(1)}, u32[]{:S(2)}, u32[]{:S(2)}) collective-permute-start(bf16[128,512]{1,0:T(8,128)(2,1)S(1)} %get-tuple-element.46.refs_2_), channel_id=1, source_target_pairs={{0,7},{1,0},{2,1},{3,2},{4,3},{5,4},{6,5},{7,6},{8,15},{9,8},{10,9... | collective-permute-start | bytes 393224 | tf_op jit(solution)/shard_map/ppermute | solution.py:362
  134.9 7.3 %collective-permute-start.21 = (bf16[128,512]{1,0:T(8,128)(2,1)S(1)}, bf16[128,512]{1,0:T(8,128)(2,1)S(1)}, u32[]{:S(2)}, u32[]{:S(2)}) collective-permute-start(bf16[128,512]{1,0:T(8,128)(2,1)S(1)} %get-tuple-element.52.refs_10_), channel_id=1, source_target_pairs={{0,1},{1,2},{2,3},{3,4},{4,5},{5,6},{6,7},{7,0},{8,9},{9,10},{10,1... | collective-permute-start | bytes 393224 | tf_op jit(solution)/shard_map/ppermute | solution.py:362
  140.5 6.7 %collective-permute-start.17 = (bf16[128,512]{1,0:T(8,128)(2,1)S(1)}, bf16[128,512]{1,0:T(8,128)(2,1)S(1)}, u32[]{:S(2)}, u32[]{:S(2)}) collective-permute-start(bf16[128,512]{1,0:T(8,128)(2,1)S(1)} %collective-permute-done.15.refs_7_), channel_id=1, source_target_pairs={{0,7},{1,0},{2,1},{3,2},{4,3},{5,4},{6,5},{7,6},{8,15},{9,8},{10,9... | collective-permute-start | bytes 393224 | tf_op jit(solution)/shard_map/ppermute | solution.py:362
  143.9 7.3 %collective-permute-start.24 = (bf16[128,512]{1,0:T(8,128)(2,1)S(1)}, bf16[128,512]{1,0:T(8,128)(2,1)S(1)}, u32[]{:S(2)}, u32[]{:S(2)}) collective-permute-start(bf16[128,512]{1,0:T(8,128)(2,1)S(1)} %collective-permute-done.22.refs_14_), channel_id=1, source_target_pairs={{0,7},{1,0},{2,1},{3,2},{4,3},{5,4},{6,5},{7,6},{8,15},{9,8},{10,9... | collective-permute-start | bytes 393224 | tf_op jit(solution)/shard_map/ppermute | solution.py:362
  147.2 7.2 %collective-permute-start.18 = (bf16[128,512]{1,0:T(8,128)(2,1)S(1)}, bf16[128,512]{1,0:T(8,128)(2,1)S(1)}, u32[]{:S(2)}, u32[]{:S(2)}) collective-permute-start(bf16[128,512]{1,0:T(8,128)(2,1)S(1)} %collective-permute-done.16.refs_4_), channel_id=1, source_target_pairs={{0,1},{1,2},{2,3},{3,4},{4,5},{5,6},{6,7},{7,0},{8,9},{9,10},{10,1... | collective-permute-start | bytes 393224 | tf_op jit(solution)/shard_map/ppermute | solution.py:362
  147.2 7.5 %collective-permute-start.19 = (bf16[128,512]{1,0:T(8,128)(2,1)S(1)}, bf16[128,512]{1,0:T(8,128)(2,1)S(1)}, u32[]{:S(2)}, u32[]{:S(2)}) collective-permute-start(bf16[128,512]{1,0:T(8,128)(2,1)S(1)} %collective-permute-done.17.refs_8_), channel_id=1, source_target_pairs={{0,7},{1,0},{2,1},{3,2},{4,3},{5,4},{6,5},{7,6},{8,15},{9,8},{10,9... | collective-permute-start | bytes 393224 | tf_op jit(solution)/shard_map/ppermute | solution.py:362
  171.7 40.5 %all-to-all-start.1 = ((bf16[32,72,512]{2,1,0:T(8,128)(2,1)}), bf16[32,72,512]{2,1,0:T(8,128)(2,1)}, u32[]{:S(2)}, u32[]{:S(2)}) async-start(bf16[32,72,512]{2,1,0:T(8,128)(2,1)} %bitcast.24), calls=%async_computation.1 | async-start | bytes 4718592 | tf_op jit(solution)/shard_map/all_to_all | solution.py:441
  (37 other events, 773.9 us)
